TPU v7x, 256 devices: a whole 4x4x8 slice. The times are simulated.
256 devices in a mesh: rows: 32 (over z, x), far: 8 (over y, core).
Axes of the slice: x: 4, y: 4, z: 8, core: 2. Of those that a mesh axis runs over, the one named last changes fastest.
Arguments:
- right_side: float32 [65536, 256], P('rows'), may hold values from -24 to 24
- near_blocks: float32 [512, 48, 128, 128], P('rows', 'far'), may hold values from -0.0234375 to 0.0234375
- near_cols: int32 [512, 48], P('rows', 'far'), may hold values from 0 to 511, as said below
- far_src: int32 [32, 32, 8], P('rows', None, 'far'), may hold values from 0 to 15
- far_tgt: int32 [32, 32, 8], P('rows', None, 'far'), may hold values from 0 to 15
- far_left: float32 [32, 32, 8, 128, 64], P('rows', None, 'far'), may hold values from -0.0546875 to 0.0546875
- far_right: float32 [32, 32, 8, 128, 64], P('rows', None, 'far'), may hold values from -0.5 to 0.5
Outputs:
- solution: float32 [65536, 256], P('rows', 'far')
- residual: float32 [65536, 256], P('rows', 'far')
Inputs may be any that keep to these rules, and one draw needn't show every extreme that they name: `near_cols`: each near-field column lies within 8 clusters of its row; slot 0 of row i names i itself, slot 1 names min(i + 8, 511) and slot 2 names max(i - 8, 0).
All inputs are finite; a program needn't handle non-finite values.
Results may differ from a plain program's by a relative error of at most 0.0003.
Values sent between devices are 32-bit elements; how exact they have to be, the bound alone decides.
A program may use at most 128 MiB of HBM per device.

v0:
```python
import jax
import jax.numpy as jnp
from jax import lax
from jax.sharding import PartitionSpec as P

B = 128
CL_DEV = 16
REACH = 8


TOP_PRECISION = lax.Precision.HIGHEST
EPS = 1e-06


def with_halo(cells, sides, width):
    for axis, dim in sides:
        count = lax.axis_size(axis)
        ends = count - 1
        head = lax.slice_in_dim(cells, 0, width, axis=dim)
        tail = lax.slice_in_dim(cells, cells.shape[dim] - width, cells.shape[dim], axis=dim)
        cells = jnp.concatenate(
            [
                lax.ppermute(tail, axis, [(i, (i + 1) % count) for i in range(ends)]),
                cells,
                lax.ppermute(head, axis, [((i + 1) % count, i) for i in range(ends)]),
            ],
            axis=dim,
        )
    return cells


def column_dots(left_vec, right_vector):
    return jnp.sum(left_vec * right_vector, axis=0)


def near_term(vector_in, near_blocks, near_cols):
    rhs_count = vector_in.shape[1]
    padded = with_halo(vector_in, (("rows", 0),), REACH * B)
    clusters = padded.reshape(-1, B, rhs_count)
    offset = lax.axis_index("rows") * CL_DEV - REACH
    picked = jnp.take(clusters, near_cols - offset, axis=0)
    return jnp.einsum("cspq,csqn->cpn", near_blocks, picked, precision=TOP_PRECISION)


def far_term(vector_in, far_src, far_tgt, far_left, far_right):
    clusters = vector_in.reshape(CL_DEV, B, vector_in.shape[1])
    picked = jnp.take(clusters, far_src[0], axis=0)
    coefficients = jnp.einsum("tsbr,tsbn->tsrn", far_right[0], picked, precision=TOP_PRECISION)
    owning_devices = (far_tgt[0][:, :, None] == jnp.arange(CL_DEV, dtype=jnp.int32)).astype(
        jnp.float32
    )
    contribution_part = jnp.einsum(
        "asbr,asrn->asbn",
        far_left[0],
        lax.all_to_all(coefficients, "rows", split_axis=0, concat_axis=0, tiled=True),
        precision=TOP_PRECISION,
    )
    return jnp.einsum("hyo,hyze->oze", owning_devices, contribution_part, precision=TOP_PRECISION)


def own_columns(vector_in):
    share_width = vector_in.shape[-1] // lax.axis_size("far")
    return lax.dynamic_slice_in_dim(
        vector_in, lax.axis_index("far") * share_width, share_width, vector_in.ndim - 1
    )


def least_squares(rhs_length, upper_left, lower_left, column_two, lower_right):
    radius_one = jnp.sqrt(upper_left * upper_left + lower_left * lower_left)
    cosine_one = upper_left / radius_one
    sine_one = lower_left / radius_one
    rotated_top = cosine_one * rhs_length
    rotated_mid = -sine_one * rhs_length
    coupled = cosine_one * column_two[0] + sine_one * column_two[1]
    diagonal_two = cosine_one * column_two[1] - sine_one * column_two[0]
    radius_two = jnp.sqrt(diagonal_two * diagonal_two + lower_right * lower_right)
    weight_two = diagonal_two * rotated_mid / (radius_two * radius_two)
    weight_one = (rotated_top - coupled * weight_two) / radius_one
    return (weight_one, weight_two)


def shards(right_side, near_blocks, near_cols, far_src, far_tgt, far_left, far_right):

    def partial_image(vector_in):
        near_part = near_term(vector_in, near_blocks, near_cols)
        far_part = far_term(vector_in, far_src, far_tgt, far_left, far_right)
        return (near_part + far_part).reshape(vector_in.shape)

    def finish(vector_in):
        return own_columns(vector_in)

    def apply_op(vector_in):
        return 0.5 * vector_in + lax.psum(partial_image(vector_in), "far")

    def orthogonal(vectors, candidate):
        heights = lax.psum(jnp.stack([column_dots(item, candidate) for item in vectors]), "rows")
        for slot_id in range(len(vectors)):
            candidate = candidate - heights[slot_id] * vectors[slot_id]
        length = jnp.sqrt(lax.psum(column_dots(candidate, candidate), "rows") + EPS)
        return (heights, candidate, length)

    rhs_length = jnp.sqrt(lax.psum(column_dots(right_side, right_side), "rows") + EPS)
    first_full = right_side / rhs_length
    image_one = apply_op(first_full)
    heights_one, candidate, lower_left = orthogonal((first_full,), image_one)
    second_vec = candidate / lower_left
    image_two = apply_op(second_vec)
    heights_two, candidate, lower_right = orthogonal((first_full, second_vec), image_two)
    weight_one, weight_two = least_squares(
        rhs_length, heights_one[0], lower_left, heights_two, lower_right
    )
    own_solution = weight_one * first_full + weight_two * second_vec
    own_residual = right_side - weight_one * image_one - weight_two * image_two
    return (finish(own_solution), finish(own_residual))


def solution(mesh):
    return jax.shard_map(
        shards,
        mesh=mesh,
        in_specs=(
            P("rows", None),
            P("rows", "far", None, None),
            P("rows", "far"),
            P("rows", None, "far"),
            P("rows", None, "far"),
            P("rows", None, "far", None, None),
            P("rows", None, "far", None, None),
        ),
        out_specs=(P("rows", "far"), P("rows", "far")),
        check_vma=False,
    )
```

profile of v0, /device:TPU:24, one launch (start us, length us, event | category | flops | bytes accessed | tf_op | source)
XLA Modules:
  0.0 807.9 jit_solution(4049094716238253556)
XLA Ops:
  12.4 77.7 %psum.49 = f32[256]{0:T(256)S(1)} all-reduce(f32[256]{0:T(256)S(1)} %multiply_reduce_fusion.5), channel_id=1, replica_groups=mesh['rows'=32,'far'=8] {'rows'}, use_global_device_ids=true, to_apply=%region_1.0 | all-reduce | flops 256 | bytes 2048 | tf_op jit(solution)/shard_map/psum | solution.py:102
  99.0 6.5 fusion.18
  105.5 4.8 all-to-all-start
  119.8 23.8 %collective-permute-done = f32[1024,256]{0,1:T(8,128)} collective-permute-done((f32[1024,256]{0,1:T(8,128)}, f32[1024,256]{0,1:T(8,128)}, u32[]{:S(2)}, u32[]{:S(2)}) %collective-permute-start) | collective-permute-done | bytes 1048608 | tf_op jit(solution)/shard_map/ppermute | solution.py:23
  147.0 4.5 pad_maximum_fusion
  151.5 5.6 copy.37
  157.1 10.9 %gather_fusion = f32[96,128,256]{2,1,0:T(8,128)} fusion(f32[32,128,256]{2,1,0:T(8,128)} %bitcast.100, s32[1024]{0:T(1024)S(1)} %pad_clamp_fusion.1), kind=kCustom, calls=%fused_computation.clone | custom fusion | bytes 25166208 | tf_op jit(solution)/shard_map/jit(_take)/gather | solution.py:41
  168.0 10.1 %convolution_bitcast_fusion.1 = f32[32,128,256]{1,2,0:T(8,128)} fusion(f32[32,1,64,256]{3,2,1,0:T(8,128)} %all-to-all-done, f32[1,32,1,128,64]{3,4,2,1,0:T(8,128)S(1)} %copy-done), kind=kOutput, calls=%fused_computation.21 | convolution fusion | flops 805306368 | bytes 7340032 | tf_op jit(solution)/shard_map/asbr,asrn->asbn/dot_general | solution.py:52
  178.1 5.5 copy.41
  187.4 21.8 %bitcast_add_fusion.1 = f32[16,128,256]{2,1,0:T(8,128)} fusion(f32[16,128,256]{2,0,1:T(8,128)S(1)} %fusion.37, f32[16,6,128,128]{3,2,1,0:T(8,128)} %param.12, f32[16,6,128,256]{3,2,1,0:T(8,128)} %bitcast.102, pred[16,6]{1,0:T(8,128)(4,1)S(1)} %copy.36), kind=kOutput, calls=%fused_computation.23 | convolution fusion | flops 4835508224 | bytes 23068768 | tf_op jit(solution)/shard_map/cspq,csqn->cpn/dot_general | solution.py:42
  212.1 86.9 %all-reduce.3.cloned.1.call-done = f32[2048,256]{0,1:T(8,128)} async-done(((f32[2048,256]{0,1:T(8,128)}), f32[2048,256]{0,1:T(8,128)}) %all-reduce.3.cloned.1.call-update) | async-done | bytes 2097168 | tf_op jit(solution)/shard_map/psum | solution.py:93
  302.4 75.0 %psum.51 = f32[256]{0:T(256)S(1)} all-reduce(f32[256]{0:T(256)S(1)} %get-tuple-element.12), channel_id=1, replica_groups=mesh['rows'=32,'far'=8] {'rows'}, use_global_device_ids=true, to_apply=%region_4.7 | all-reduce | flops 256 | bytes 2048 | tf_op jit(solution)/shard_map/psum | solution.py:96
  379.6 69.8 %psum.52 = f32[256]{0:T(256)S(1)} all-reduce(f32[256]{0:T(256)S(1)} %multiply_reduce_fusion.3), channel_id=1, replica_groups=mesh['rows'=32,'far'=8] {'rows'}, use_global_device_ids=true, to_apply=%region_6.9 | all-reduce | flops 256 | bytes 2048 | tf_op jit(solution)/shard_map/psum | solution.py:99
  460.2 6.5 fusion.21
  466.7 6.2 all-to-all-start.1
  479.7 18.0 %collective-permute-done.2 = f32[1024,256]{0,1:T(8,128)S(1)} collective-permute-done((f32[1024,256]{0,1:T(8,128)S(1)}, f32[1024,256]{0,1:T(8,128)S(1)}, u32[]{:S(2)}, u32[]{:S(2)}) %collective-permute-start.2) | collective-permute-done | bytes 1048608 | tf_op jit(solution)/shard_map/ppermute | solution.py:23
  503.3 5.8 copy.45
  509.1 10.9 %gather_fusion.2 = f32[96,128,256]{2,1,0:T(8,128)} fusion(f32[32,128,256]{2,1,0:T(8,128)} %bitcast.99, s32[1024]{0:T(1024)S(1)} %pad_clamp_fusion.1), kind=kCustom, calls=%fused_computation.2.clone | custom fusion | bytes 25166208 | tf_op jit(solution)/shard_map/jit(_take)/gather | solution.py:41
  520.0 10.1 %convolution_bitcast_fusion = f32[32,128,256]{1,2,0:T(8,128)} fusion(f32[32,1,64,256]{3,2,1,0:T(8,128)} %all-to-all-done.1, f32[1,32,1,128,64]{3,4,2,1,0:T(8,128)S(1)} %copy-done), kind=kOutput, calls=%fused_computation.20 | convolution fusion | flops 805306368 | bytes 7340032 | tf_op jit(solution)/shard_map/asbr,asrn->asbn/dot_general | solution.py:52
  530.1 5.5 copy.49
  539.3 21.5 %bitcast_add_fusion = f32[16,128,256]{2,1,0:T(8,128)} fusion(f32[16,128,256]{2,0,1:T(8,128)S(1)} %fusion.35, f32[16,6,128,128]{3,2,1,0:T(8,128)} %param.12, f32[16,6,128,256]{3,2,1,0:T(8,128)} %bitcast.101, pred[16,6]{1,0:T(8,128)(4,1)S(1)} %copy.36), kind=kOutput, calls=%fused_computation.22 | convolution fusion | flops 4835508224 | bytes 23068768 | tf_op jit(solution)/shard_map/cspq,csqn->cpn/dot_general | solution.py:42
  563.8 83.1 %all-reduce.5.cloned.1.call-done = f32[2048,256]{0,1:T(8,128)} async-done(((f32[2048,256]{0,1:T(8,128)}), f32[2048,256]{0,1:T(8,128)}) %all-reduce.5.cloned.1.call-update) | async-done | bytes 2097168 | tf_op jit(solution)/shard_map/psum | solution.py:93
  650.9 75.1 %psum.54 = f32[2,256]{1,0:T(2,128)S(1)} all-reduce(f32[2,256]{1,0:T(2,128)S(1)} %pad_maximum_fusion.2), channel_id=1, replica_groups=mesh['rows'=32,'far'=8] {'rows'}, use_global_device_ids=true, to_apply=%region_10.13 | all-reduce | flops 512 | bytes 4096 | tf_op jit(solution)/shard_map/psum | solution.py:96
  728.8 69.6 %psum.55 = f32[256]{0:T(256)S(1)} all-reduce(f32[256]{0:T(256)S(1)} %multiply_reduce_fusion), channel_id=1, replica_groups=mesh['rows'=32,'far'=8] {'rows'}, use_global_device_ids=true, to_apply=%region_12.15 | all-reduce | flops 256 | bytes 2048 | tf_op jit(solution)/shard_map/psum | solution.py:99
  (55 shorter events, 78.3 us)
Async XLA Ops:
  7.2 160.9 %copy-start = (f32[1,32,1,128,64]{3,4,2,1,0:T(8,128)S(1)}, f32[1,32,1,128,64]{3,4,2,1,0:T(8,128)}, u32[]{:S(2)}) copy-start(f32[1,32,1,128,64]{3,4,2,1,0:T(8,128)} %param.16) | copy-start | bytes 3145732
  105.5 62.6 %all-to-all-start = ((f32[32,1,64,256]{3,2,1,0:T(8,128)}), f32[32,1,64,256]{3,2,1,0:T(8,128)}, u32[]{:S(2)}, u32[]{:S(2)}) async-start(f32[32,1,64,256]{3,2,1,0:T(8,128)} %fusion.18), calls=%async_computation | async-start | bytes 4194304 | tf_op jit(solution)/shard_map/all_to_all | solution.py:55
  110.2 9.3 %copy-start.2 = (s32[16,6]{0,1:T(8,128)S(1)}, s32[16,6]{0,1:T(8,128)}, u32[]{:S(2)}) copy-start(s32[16,6]{0,1:T(8,128)} %param.13) | copy-start | bytes 1156
  110.2 188.8 %all-reduce.3.cloned.1.call-start = ((), (), s32[]{:S(2)}) async-start(), calls=%async_computation.2 | async-start | bytes 4194304 | tf_op jit(solution)/shard_map/psum | solution.py:93
  113.4 30.2 %collective-permute-start = (f32[1024,256]{0,1:T(8,128)}, f32[1024,256]{0,1:T(8,128)}, u32[]{:S(2)}, u32[]{:S(2)}) collective-permute-start(f32[1024,256]{0,1:T(8,128)} %get-tuple-element.15), channel_id=1, source_target_pairs={{0,8},{8,16},{16,24},{24,32},{32,40},{40,48},{48,56},{56,64},{64,7... | collective-permute-start | bytes 3145736 | tf_op jit(solution)/shard_map/ppermute | solution.py:23
  118.0 29.0 %collective-permute-start.1 = (f32[1024,256]{0,1:T(8,128)}, f32[1024,256]{0,1:T(8,128)}, u32[]{:S(2)}, u32[]{:S(2)}) collective-permute-start(f32[1024,256]{0,1:T(8,128)} %get-tuple-element.16), channel_id=1, source_target_pairs={{8,0},{16,8},{24,16},{32,24},{40,32},{48,40},{56,48},{64,56},{72,6... | collective-permute-start | bytes 3145736 | tf_op jit(solution)/shard_map/ppermute | solution.py:25
  178.1 5.5 copy-start.3
  466.7 53.3 %all-to-all-start.1 = ((f32[32,1,64,256]{3,2,1,0:T(8,128)}), f32[32,1,64,256]{3,2,1,0:T(8,128)}, u32[]{:S(2)}, u32[]{:S(2)}) async-start(f32[32,1,64,256]{3,2,1,0:T(8,128)} %fusion.21), calls=%async_computation.1 | async-start | bytes 4194304 | tf_op jit(solution)/shard_map/all_to_all | solution.py:55
  472.8 174.1 %all-reduce.5.cloned.1.call-start = ((), (), s32[]{:S(2)}) async-start(), calls=%async_computation.3 | async-start | bytes 4194304 | tf_op jit(solution)/shard_map/psum | solution.py:93
  472.9 28.1 %copy-start.1 = (f32[2048,256]{0,1:T(8,128)S(1)}, f32[2048,256]{0,1:T(8,128)}, u32[]{:S(2)}) copy-start(f32[2048,256]{0,1:T(8,128)} %broadcast_divide_fusion) | copy-start | bytes 6291460
  474.7 22.9 %collective-permute-start.2 = (f32[1024,256]{0,1:T(8,128)S(1)}, f32[1024,256]{0,1:T(8,128)S(1)}, u32[]{:S(2)}, u32[]{:S(2)}) collective-permute-start(f32[1024,256]{0,1:T(8,128)S(1)} %get-tuple-element.13), channel_id=1, source_target_pairs={{0,8},{8,16},{16,24},{24,32},{32,40},{40,48},{48,56},{56,64},{64,7... | collective-permute-start | bytes 3145736 | tf_op jit(solution)/shard_map/ppermute | solution.py:23
  478.4 22.6 %collective-permute-start.3 = (f32[1024,256]{0,1:T(8,128)S(1)}, f32[1024,256]{0,1:T(8,128)S(1)}, u32[]{:S(2)}, u32[]{:S(2)}) collective-permute-start(f32[1024,256]{0,1:T(8,128)S(1)} %get-tuple-element.14), channel_id=1, source_target_pairs={{8,0},{16,8},{24,16},{32,24},{40,32},{48,40},{56,48},{64,56},{72,6... | collective-permute-start | bytes 3145736 | tf_op jit(solution)/shard_map/ppermute | solution.py:25
Sparse Core Ops, SparseCore 0:
  212.2 86.7 all-reduce.2
  563.9 82.9 all-reduce.4
where the time goes:
time: 817 us; the launch traced here: 808 us
  blocking collectives  367 us (45%)
  waiting for transfers between devices  219 us (27%)
  matrix products  83.9 us (10%)
  local copies, waits for them, and re-layouts  71.9 us (9%)
  other arithmetic  29.8 us (4%)
  starting transfers between devices  22.1 us (3%)
  between operations  14.5 us (2%)
    psum x2, waiting for transfers between devices, apply_op(): return 0.5 * vector_in + lax.psum(partial_image(vector_in), 'far')  170 us
    psum x2, blocking collectives, orthogonal(): lax.psum(jnp.stack([column_dots(item, candidate) for item in vectors]), '...  150 us
    psum x2, blocking collectives, orthogonal(): length = jnp.sqrt(lax.psum(column_dots(candidate, candidate), 'rows') + EPS)  139 us
    psum x1, blocking collectives, shards(): lax.psum(column_dots(right_side, right_side), 'rows') + EPS  77.7 us
    dot_general x2, matrix products, near_term(): jnp.einsum('cspq,csqn->cpn', near_blocks, picked, precision=TOP_PRECISION)  43.3 us
    ppermute x2, waiting for transfers between devices, with_halo(): lax.ppermute(tail, axis, [(i, (i + 1) % count) for i in range(ends)])  41.8 us
    gather x2, local copies, waits for them, and re-layouts, near_term(): picked = jnp.take(clusters, near_cols - offset, axis=0)  21.8 us
    dot_general x2, matrix products, far_term(): jnp.einsum('asbr,asrn->asbn', far_left[0], lax.all_to_all(coefficients, '...  20.1 us
  transfers between devices with their start and end apart: 8, of which 6 were waited for; matrix products, arithmetic and copies ran while one was open for 6% of the time, Pallas kernels for 0%

commit v1 on v0

--- a/solution.py
+++ b/solution.py
@@ -65,18 +65,42 @@
     )
 
 
-def least_squares(rhs_length, upper_left, lower_left, column_two, lower_right):
+def combine(gram):
+    bb, bu, uu, bw, uw, ww = gram
+    length_sq = bb + EPS
+    length = jnp.sqrt(length_sq)
+    unit = bb / length_sq
+    gap = EPS / length_sq
+    p1, q11, p2, q12, q22 = bu / length_sq, uu / length_sq, bw / length_sq, uw / length_sq, ww / length_sq
+    upper_left = 0.5 * unit + p1
+    alpha = p1 - 0.5 * gap
+    cand_sq = jnp.maximum(q11 - 2.0 * alpha * p1 + alpha * alpha * unit, 0.0)
+    lower_sq = cand_sq + EPS
+    lower_left = jnp.sqrt(lower_sq)
+    f_s = (p1 - alpha * unit) / lower_left
+    f_ns = (p2 - alpha * p1) / lower_left
+    s_s = cand_sq / lower_sq
+    s_ns = (q12 - alpha * q11 - alpha * p2 + alpha * alpha * p1) / lower_sq
+    ns_ns = (q22 - 2.0 * alpha * q12 + alpha * alpha * q11) / lower_sq
+    top = 0.5 * f_s + f_ns
+    mid = 0.5 * s_s + s_ns
+    beta = s_ns - 0.5 * EPS / lower_sq
+    rest_sq = ns_ns + top * top * unit + beta * beta * s_s - 2.0 * top * f_ns - 2.0 * beta * s_ns + 2.0 * top * beta * f_s
+    lower_right = jnp.sqrt(jnp.maximum(rest_sq, 0.0) + EPS)
     radius_one = jnp.sqrt(upper_left * upper_left + lower_left * lower_left)
     cosine_one = upper_left / radius_one
     sine_one = lower_left / radius_one
-    rotated_top = cosine_one * rhs_length
-    rotated_mid = -sine_one * rhs_length
-    coupled = cosine_one * column_two[0] + sine_one * column_two[1]
-    diagonal_two = cosine_one * column_two[1] - sine_one * column_two[0]
+    rotated_top = cosine_one * length
+    rotated_mid = -sine_one * length
+    coupled = cosine_one * top + sine_one * mid
+    diagonal_two = cosine_one * mid - sine_one * top
     radius_two = jnp.sqrt(diagonal_two * diagonal_two + lower_right * lower_right)
     weight_two = diagonal_two * rotated_mid / (radius_two * radius_two)
     weight_one = (rotated_top - coupled * weight_two) / radius_one
-    return (weight_one, weight_two)
+    one = weight_one / length
+    two = weight_two / (lower_left * length)
+    sol_b = one - alpha * two
+    return sol_b, two, 1.0 - 0.5 * sol_b, -0.5 * two - one + alpha * two, -two
 
 
 def shards(right_side, near_blocks, near_cols, far_src, far_tgt, far_left, far_right):
@@ -86,32 +110,14 @@
         far_part = far_term(vector_in, far_src, far_tgt, far_left, far_right)
         return (near_part + far_part).reshape(vector_in.shape)
 
-    def finish(vector_in):
-        return own_columns(vector_in)
-
-    def apply_op(vector_in):
-        return 0.5 * vector_in + lax.psum(partial_image(vector_in), "far")
-
-    def orthogonal(vectors, candidate):
-        heights = lax.psum(jnp.stack([column_dots(item, candidate) for item in vectors]), "rows")
-        for slot_id in range(len(vectors)):
-            candidate = candidate - heights[slot_id] * vectors[slot_id]
-        length = jnp.sqrt(lax.psum(column_dots(candidate, candidate), "rows") + EPS)
-        return (heights, candidate, length)
-
-    rhs_length = jnp.sqrt(lax.psum(column_dots(right_side, right_side), "rows") + EPS)
-    first_full = right_side / rhs_length
-    image_one = apply_op(first_full)
-    heights_one, candidate, lower_left = orthogonal((first_full,), image_one)
-    second_vec = candidate / lower_left
-    image_two = apply_op(second_vec)
-    heights_two, candidate, lower_right = orthogonal((first_full, second_vec), image_two)
-    weight_one, weight_two = least_squares(
-        rhs_length, heights_one[0], lower_left, heights_two, lower_right
-    )
-    own_solution = weight_one * first_full + weight_two * second_vec
-    own_residual = right_side - weight_one * image_one - weight_two * image_two
-    return (finish(own_solution), finish(own_residual))
+    image_one = lax.psum(partial_image(right_side), "far")
+    own_two = lax.psum_scatter(partial_image(image_one), "far", scatter_dimension=1, tiled=True)
+    own_side = own_columns(right_side)
+    own_one = own_columns(image_one)
+    pairs = ((own_side, own_side), (own_side, own_one), (own_one, own_one), (own_side, own_two), (own_one, own_two), (own_two, own_two))
+    gram = lax.psum(jnp.stack([column_dots(left, right) for left, right in pairs]), "rows")
+    sol_b, sol_u, res_b, res_u, res_w = combine(gram)
+    return (sol_b * own_side + sol_u * own_one, res_b * own_side + res_u * own_one + res_w * own_two)
 
 
 def solution(mesh):

time: 817 us -> 509 us (0.62)
  blocking collectives: 367 us -> 75 us
  other arithmetic: 29.8 us -> 10.8 us
  starting transfers between devices: 22.1 us -> 34.8 us
  local copies, waits for them, and re-layouts: 71.9 us -> 62.4 us
    psum x5 -> x1, blocking collectives: 367 us -> 75 us  [shards(): lax.psum(jnp.stack([column_dots(left, right) for left, right in pairs]),...]
    psum x2 -> x1, waiting for transfers between devices: 170 us -> 89.9 us  [shards(): image_one = lax.psum(partial_image(right_side), 'far')]
    ppermute x2, waiting for transfers between devices: 6.66 us -> 80.3 us  [with_halo(): lax.ppermute(head, axis, [((i + 1) % count, i) for i in range(ends)])]
    reduce_scatter x0 -> x1, waiting for transfers between devices: none -> 51.1 us  [shards(): lax.psum_scatter(partial_image(image_one), 'far', scatter_dimension=1, ti...]
    ppermute x2, waiting for transfers between devices: 41.8 us -> 0.01 us  [with_halo(): lax.ppermute(tail, axis, [(i, (i + 1) % count) for i in range(ends)])]
    all_to_all x2, starting transfers between devices: 10.9 us -> 21.5 us  [far_term(): lax.all_to_all(coefficients, 'rows', split_axis=0, concat_axis=0, tiled=T...]
    reduce_sum x4 -> x1, other arithmetic: 10.9 us -> 1.31 us  [column_dots(): return jnp.sum(left_vec * right_vector, axis=0)]
  transfers between devices with their start and end apart: 8 -> 8, of which waited for: 6 -> 4; matrix products, arithmetic and copies ran while one was open for 6% -> 8% of each run, Pallas kernels for 0% -> 0%
where the time goes in v1:
time: 509 us; the launch traced here: 503 us
  waiting for transfers between devices  221 us (43%)
  matrix products  84 us (17%)
  blocking collectives  75 us (15%)
  local copies, waits for them, and re-layouts  62.4 us (12%)
  starting transfers between devices  34.8 us (7%)
  between operations  14.4 us (3%)
  other arithmetic  10.8 us (2%)
    psum x1, waiting for transfers between devices, shards(): image_one = lax.psum(partial_image(right_side), 'far')  89.9 us
    ppermute x2, waiting for transfers between devices, with_halo(): lax.ppermute(head, axis, [((i + 1) % count, i) for i in range(ends)])  80.3 us
    psum x1, blocking collectives, shards(): lax.psum(jnp.stack([column_dots(left, right) for left, right in pairs]),...  75 us
    reduce_scatter x1, waiting for transfers between devices, shards(): lax.psum_scatter(partial_image(image_one), 'far', scatter_dimension=1, ti...  51.1 us
    dot_general x2, matrix products, near_term(): jnp.einsum('cspq,csqn->cpn', near_blocks, picked, precision=TOP_PRECISION)  43.2 us
    gather x2, local copies, waits for them, and re-layouts, near_term(): picked = jnp.take(clusters, near_cols - offset, axis=0)  21.8 us
    all_to_all x2, starting transfers between devices, far_term(): lax.all_to_all(coefficients, 'rows', split_axis=0, concat_axis=0, tiled=T...  21.5 us
    dot_general x2, matrix products, far_term(): jnp.einsum('asbr,asrn->asbn', far_left[0], lax.all_to_all(coefficients, '...  20.1 us
  transfers between devices with their start and end apart: 8, of which 4 were waited for; matrix products, arithmetic and copies ran while one was open for 8% of the time, Pallas kernels for 0%

profile of v1, /device:TPU:24, one launch (start us, length us, event | category | flops | bytes accessed | tf_op | source)
XLA Modules:
  0.0 502.8 jit_solution(17007682914107022496)
XLA Ops:
  8.6 4.3 gather_fusion.1
  12.9 6.6 %fusion.18 = f32[32,1,64,256]{3,2,1,0:T(8,128)} fusion(f32[32,128,256]{2,1,0:T(8,128)} %gather_fusion.1, pred[32]{0:T(512)(128)(4,1)S(1)} %and_bitcast_fusion, f32[1,32,1,128,64]{3,4,2,1,0:T(8,128)} %param.17), kind=kOutput, calls=%fused_computation.30 | convolution fusion | flops 806354944 | bytes 7340064 | tf_op jit(solution)/shard_map/tsbr,tsbn->tsrn/dot_general | solution.py:48
  19.6 11.6 %all-to-all-start = ((f32[32,1,64,256]{3,2,1,0:T(8,128)}), f32[32,1,64,256]{3,2,1,0:T(8,128)}, u32[]{:S(2)}, u32[]{:S(2)}) async-start(f32[32,1,64,256]{3,2,1,0:T(8,128)} %fusion.18), calls=%async_computation | async-start | bytes 4194304 | tf_op jit(solution)/shard_map/all_to_all | solution.py:55
  34.0 5.9 %collective-permute-start = (f32[1024,256]{1,0:T(8,128)}, f32[1024,256]{1,0:T(8,128)}, u32[]{:S(2)}, u32[]{:S(2)}) collective-permute-start(f32[1024,256]{1,0:T(8,128)} %get-tuple-element.27), channel_id=1, source_target_pairs={{0,8},{8,16},{16,24},{24,32},{32,40},{40,48},{48,56},{56,64},{64,7... | collective-permute-start | bytes 3145736 | tf_op jit(solution)/shard_map/ppermute | solution.py:23
  40.1 38.7 %collective-permute-done.1 = f32[1024,256]{1,0:T(8,128)} collective-permute-done((f32[1024,256]{1,0:T(8,128)}, f32[1024,256]{1,0:T(8,128)}, u32[]{:S(2)}, u32[]{:S(2)}) %collective-permute-start.1) | collective-permute-done | bytes 1048608 | tf_op jit(solution)/shard_map/ppermute | solution.py:25
  82.6 10.9 %gather_fusion = f32[96,128,256]{2,1,0:T(8,128)} fusion(f32[32,128,256]{2,1,0:T(8,128)} %bitcast.110, s32[1024]{0:T(1024)S(1)} %pad_clamp_fusion.1), kind=kCustom, calls=%fused_computation.clone | custom fusion | bytes 25166208 | tf_op jit(solution)/shard_map/jit(_take)/gather | solution.py:41
  93.6 10.1 %convolution_bitcast_fusion.1 = f32[32,128,256]{1,2,0:T(8,128)} fusion(f32[32,1,64,256]{3,2,1,0:T(8,128)} %all-to-all-done, f32[1,32,1,128,64]{3,4,2,1,0:T(8,128)S(1)} %copy-done), kind=kOutput, calls=%fused_computation.21 | convolution fusion | flops 805306368 | bytes 7340032 | tf_op jit(solution)/shard_map/asbr,asrn->asbn/dot_general | solution.py:52
  103.6 5.5 %copy.34 = f32[32,128,256]{2,0,1:T(8,128)} copy(f32[32,128,256]{1,2,0:T(8,128)} %convolution_bitcast_fusion.1) | data formatting | bytes 8388608 | tf_op jit(solution)/shard_map/asbr,asrn->asbn/dot_general | solution.py:52
  109.2 3.8 fusion.35
  112.9 21.8 %bitcast_add_fusion.1 = f32[16,128,256]{2,1,0:T(8,128)} fusion(f32[16,128,256]{2,0,1:T(8,128)S(1)} %fusion.35, f32[16,6,128,128]{3,2,1,0:T(8,128)} %param.12, f32[16,6,128,256]{3,2,1,0:T(8,128)} %bitcast.113, pred[16,6]{1,0:T(8,128)(4,1)S(1)} %copy.31), kind=kOutput, calls=%fused_computation.23 | convolution fusion | flops 4835508224 | bytes 23068768 | tf_op jit(solution)/shard_map/cspq,csqn->cpn/dot_general | solution.py:42
  137.6 89.9 %all-reduce.2.cloned.1.call-done = f32[2048,256]{0,1:T(8,128)} async-done(((f32[2048,256]{0,1:T(8,128)}), f32[2048,256]{0,1:T(8,128)}) %all-reduce.2.cloned.1.call-update) | async-done | bytes 2097168 | tf_op jit(solution)/shard_map/psum | solution.py:113
  230.4 4.3 gather_fusion.3
  234.8 6.5 %fusion.21 = f32[32,1,64,256]{3,2,1,0:T(8,128)} fusion(f32[32,128,256]{2,1,0:T(8,128)} %gather_fusion.3, pred[32]{0:T(512)(128)(4,1)S(1)} %and_bitcast_fusion, f32[1,32,1,128,64]{3,4,2,1,0:T(8,128)} %param.17), kind=kOutput, calls=%fused_computation.31 | convolution fusion | flops 806354944 | bytes 7340064 | tf_op jit(solution)/shard_map/tsbr,tsbn->tsrn/dot_general | solution.py:48
  241.3 9.9 %all-to-all-start.1 = ((f32[32,1,64,256]{3,2,1,0:T(8,128)}), f32[32,1,64,256]{3,2,1,0:T(8,128)}, u32[]{:S(2)}, u32[]{:S(2)}) async-start(f32[32,1,64,256]{3,2,1,0:T(8,128)} %fusion.21), calls=%async_computation.1 | async-start | bytes 4194304 | tf_op jit(solution)/shard_map/all_to_all | solution.py:55
  254.6 4.6 collective-permute-start.2
  259.2 41.6 %collective-permute-done.3 = f32[1024,256]{0,1:T(8,128)S(1)} collective-permute-done((f32[1024,256]{0,1:T(8,128)S(1)}, f32[1024,256]{0,1:T(8,128)S(1)}, u32[]{:S(2)}, u32[]{:S(2)}) %collective-permute-start.3) | collective-permute-done | bytes 1048608 | tf_op jit(solution)/shard_map/ppermute | solution.py:25
  303.0 5.6 %copy.38 = f32[4096,256]{1,0:T(8,128)} copy(f32[4096,256]{0,1:T(8,128)} %pad_maximum_fusion.1) | data formatting | bytes 8388608 | tf_op jit(solution)/shard_map/concatenate | solution.py:21
  308.6 10.9 %gather_fusion.2 = f32[96,128,256]{2,1,0:T(8,128)} fusion(f32[32,128,256]{2,1,0:T(8,128)} %bitcast.111, s32[1024]{0:T(1024)S(1)} %pad_clamp_fusion.1), kind=kCustom, calls=%fused_computation.2.clone | custom fusion | bytes 25166208 | tf_op jit(solution)/shard_map/jit(_take)/gather | solution.py:41
  319.5 10.1 %convolution_bitcast_fusion = f32[32,128,256]{1,2,0:T(8,128)} fusion(f32[32,1,64,256]{3,2,1,0:T(8,128)} %all-to-all-done.1, f32[1,32,1,128,64]{3,4,2,1,0:T(8,128)S(1)} %copy-done), kind=kOutput, calls=%fused_computation.20 | convolution fusion | flops 805306368 | bytes 7340032 | tf_op jit(solution)/shard_map/asbr,asrn->asbn/dot_general | solution.py:52
  329.6 5.5 %copy.42 = f32[32,128,256]{2,0,1:T(8,128)} copy(f32[32,128,256]{1,2,0:T(8,128)} %convolution_bitcast_fusion) | data formatting | bytes 8388608 | tf_op jit(solution)/shard_map/asbr,asrn->asbn/dot_general | solution.py:52
  335.1 3.8 fusion.33
  338.9 21.5 %bitcast_add_fusion = f32[16,128,256]{2,1,0:T(8,128)} fusion(f32[16,128,256]{2,0,1:T(8,128)S(1)} %fusion.33, f32[16,6,128,128]{3,2,1,0:T(8,128)} %param.12, f32[16,6,128,256]{3,2,1,0:T(8,128)} %bitcast.112, pred[16,6]{1,0:T(8,128)(4,1)S(1)} %copy.31), kind=kOutput, calls=%fused_computation.22 | convolution fusion | flops 4835508224 | bytes 23068768 | tf_op jit(solution)/shard_map/cspq,csqn->cpn/dot_general | solution.py:42
  366.2 51.1 %reduce-scatter.2.cloned.1.call-done = f32[2048,32]{0,1:T(8,128)} async-done(((f32[2048,256]{0,1:T(8,128)}), f32[2048,32]{0,1:T(8,128)}) %reduce-scatter.2.cloned.1.call-update) | async-done | bytes 262160 | tf_op jit(solution)/shard_map/reduce_scatter | solution.py:114
  418.6 75.0 %psum.15 = f32[6,32]{1,0:T(8,128)S(1)} all-reduce(f32[6,32]{1,0:T(8,128)S(1)} %stack.27), channel_id=1, replica_groups=mesh['rows'=32,'far'=8] {'rows'}, use_global_device_ids=true, to_apply=%region_8.11 | all-reduce | flops 192 | bytes 1536 | tf_op jit(solution)/shard_map/psum | solution.py:118
  (43 shorter events, 28.9 us)
Async XLA Ops:
  7.2 86.4 %copy-start = (f32[1,32,1,128,64]{3,4,2,1,0:T(8,128)S(1)}, f32[1,32,1,128,64]{3,4,2,1,0:T(8,128)}, u32[]{:S(2)}) copy-start(f32[1,32,1,128,64]{3,4,2,1,0:T(8,128)} %param.16) | copy-start | bytes 3145732
  12.9 18.3 %copy-start.1 = (f32[2048,256]{1,0:T(8,128)S(1)}, f32[2048,256]{1,0:T(8,128)}, u32[]{:S(2)}) copy-start(f32[2048,256]{1,0:T(8,128)} %param.11) | copy-start | bytes 6291460
  19.6 20.2 %copy-start.3 = (s32[16,6]{0,1:T(8,128)S(1)}, s32[16,6]{0,1:T(8,128)}, u32[]{:S(2)}) copy-start(s32[16,6]{0,1:T(8,128)} %param.13) | copy-start | bytes 1156
  19.6 74.0 %all-to-all-start = ((f32[32,1,64,256]{3,2,1,0:T(8,128)}), f32[32,1,64,256]{3,2,1,0:T(8,128)}, u32[]{:S(2)}, u32[]{:S(2)}) async-start(f32[32,1,64,256]{3,2,1,0:T(8,128)} %fusion.18), calls=%async_computation | async-start | bytes 4194304 | tf_op jit(solution)/shard_map/all_to_all | solution.py:55
  31.2 196.4 %all-reduce.2.cloned.1.call-start = ((), (), s32[]{:S(2)}) async-start(), calls=%async_computation.3 | async-start | bytes 4194304 | tf_op jit(solution)/shard_map/psum | solution.py:113
  32.7 46.2 %collective-permute-start.1 = (f32[1024,256]{1,0:T(8,128)}, f32[1024,256]{1,0:T(8,128)}, u32[]{:S(2)}, u32[]{:S(2)}) collective-permute-start(f32[1024,256]{1,0:T(8,128)} %get-tuple-element.28), channel_id=1, source_target_pairs={{8,0},{16,8},{24,16},{32,24},{40,32},{48,40},{56,48},{64,56},{72,6... | collective-permute-start | bytes 3145736 | tf_op jit(solution)/shard_map/ppermute | solution.py:25
  34.0 44.9 %collective-permute-start = (f32[1024,256]{1,0:T(8,128)}, f32[1024,256]{1,0:T(8,128)}, u32[]{:S(2)}, u32[]{:S(2)}) collective-permute-start(f32[1024,256]{1,0:T(8,128)} %get-tuple-element.27), channel_id=1, source_target_pairs={{0,8},{8,16},{16,24},{24,32},{32,40},{40,48},{48,56},{56,64},{64,7... | collective-permute-start | bytes 3145736 | tf_op jit(solution)/shard_map/ppermute | solution.py:23
  103.6 5.5 %copy-start.4 = (s32[1,32,1]{1,2,0:T(1,128)S(1)}, s32[1,32,1]{1,2,0:T(1,128)}, u32[]{:S(2)}) copy-start(s32[1,32,1]{1,2,0:T(1,128)} %param.15) | copy-start | bytes 388
  241.3 78.3 %all-to-all-start.1 = ((f32[32,1,64,256]{3,2,1,0:T(8,128)}), f32[32,1,64,256]{3,2,1,0:T(8,128)}, u32[]{:S(2)}, u32[]{:S(2)}) async-start(f32[32,1,64,256]{3,2,1,0:T(8,128)} %fusion.21), calls=%async_computation.1 | async-start | bytes 4194304 | tf_op jit(solution)/shard_map/all_to_all | solution.py:55
  251.2 166.0 %reduce-scatter.2.cloned.1.call-start = ((), (), s32[]{:S(2)}) async-start(), calls=%async_computation.4 | async-start | bytes 2359296 | tf_op jit(solution)/shard_map/reduce_scatter | solution.py:114
  251.4 49.3 %copy-start.2 = (f32[2048,256]{0,1:T(8,128)S(1)}, f32[2048,256]{0,1:T(8,128)}, u32[]{:S(2)}) copy-start(f32[2048,256]{0,1:T(8,128)} %all-reduce.2.cloned.1.call-done) | copy-start | bytes 6291460
  253.3 47.5 %collective-permute-start.3 = (f32[1024,256]{0,1:T(8,128)S(1)}, f32[1024,256]{0,1:T(8,128)S(1)}, u32[]{:S(2)}, u32[]{:S(2)}) collective-permute-start(f32[1024,256]{0,1:T(8,128)S(1)} %get-tuple-element.26), channel_id=1, source_target_pairs={{8,0},{16,8},{24,16},{32,24},{40,32},{48,40},{56,48},{64,56},{72,6... | collective-permute-start | bytes 3145736 | tf_op jit(solution)/shard_map/ppermute | solution.py:25
  254.6 46.2 %collective-permute-start.2 = (f32[1024,256]{0,1:T(8,128)S(1)}, f32[1024,256]{0,1:T(8,128)S(1)}, u32[]{:S(2)}, u32[]{:S(2)}) collective-permute-start(f32[1024,256]{0,1:T(8,128)S(1)} %get-tuple-element.25), channel_id=1, source_target_pairs={{0,8},{8,16},{16,24},{24,32},{32,40},{40,48},{48,56},{56,64},{64,7... | collective-permute-start | bytes 3145736 | tf_op jit(solution)/shard_map/ppermute | solution.py:23
Sparse Core Ops, SparseCore 0:
  137.8 89.7 all-reduce.1
  363.5 53.7 reduce-scatter.1

commit v2 on v1

v2 whole, which is shorter than its diff:
```python
import functools

import jax
import jax.numpy as jnp
from jax import lax
from jax.experimental import pallas as pl
from jax.experimental.pallas import tpu as pltpu
from jax.sharding import PartitionSpec as P

B = 128
R = 64
HALF = 128
NEAR_DEV = 6
CL_DEV = 16
ROW_X = 4
FAR_Y = 4
EPS = 1e-06
MESH = pl.DeviceIdType.MESH
F32 = jnp.float32
BF16 = jnp.bfloat16


def split(value):
    high = value.astype(BF16)
    return high, (value - high.astype(F32)).astype(BF16)


def quadrants(value):
    rows = value.shape[0] // 2
    return (value[:rows, :HALF] + value[:rows, HALF:]) + (value[rows:, :HALF] + value[rows:, HALF:])


def combine(gram):
    bb, bu, uu, bw, uw, ww = gram
    length_sq = bb + EPS
    length = jnp.sqrt(length_sq)
    unit = bb / length_sq
    gap = EPS / length_sq
    p1, q11, p2, q12, q22 = bu / length_sq, uu / length_sq, bw / length_sq, uw / length_sq, ww / length_sq
    upper_left = 0.5 * unit + p1
    alpha = p1 - 0.5 * gap
    cand_sq = jnp.maximum(q11 - 2.0 * alpha * p1 + alpha * alpha * unit, 0.0)
    lower_sq = cand_sq + EPS
    lower_left = jnp.sqrt(lower_sq)
    f_s = (p1 - alpha * unit) / lower_left
    f_ns = (p2 - alpha * p1) / lower_left
    s_s = cand_sq / lower_sq
    s_ns = (q12 - alpha * q11 - alpha * p2 + alpha * alpha * p1) / lower_sq
    ns_ns = (q22 - 2.0 * alpha * q12 + alpha * alpha * q11) / lower_sq
    top = 0.5 * f_s + f_ns
    mid = 0.5 * s_s + s_ns
    beta = s_ns - 0.5 * EPS / lower_sq
    rest_sq = ns_ns + top * top * unit + beta * beta * s_s - 2.0 * top * f_ns - 2.0 * beta * s_ns + 2.0 * top * beta * f_s
    lower_right = jnp.sqrt(jnp.maximum(rest_sq, 0.0) + EPS)
    radius_one = jnp.sqrt(upper_left * upper_left + lower_left * lower_left)
    cosine_one = upper_left / radius_one
    sine_one = lower_left / radius_one
    rotated_top = cosine_one * length
    rotated_mid = -sine_one * length
    coupled = cosine_one * top + sine_one * mid
    diagonal_two = cosine_one * mid - sine_one * top
    radius_two = jnp.sqrt(diagonal_two * diagonal_two + lower_right * lower_right)
    weight_two = diagonal_two * rotated_mid / (radius_two * radius_two)
    weight_one = (rotated_top - coupled * weight_two) / radius_one
    one = weight_one / length
    two = weight_two / (lower_left * length)
    sol_b = one - alpha * two
    return sol_b, two, 1.0 - 0.5 * sol_b, -0.5 * two - one + alpha * two, -two


def kernel(
    n_rows,
    cols_ref, src_ref, tgt_ref, side_hbm, near_hbm, left_hbm, right_hbm,
    sol_ref, res_ref,
    side, near_raw, near, left_raw, left, right_raw, right, vcat, coef_out, coef_in,
    halo_b, own_u, halo_u, acc, chain, part, part_t,
    sib_in, mix, y_in, sib_t, mix_t, y_t, turned, own_w, gram_out, gram_in,
    prev, last,
    load_sem, a2a_s, a2a_r, halo_s, halo_r, agy_s, agy_r, ags_s, ags_r,
    rss_s, rss_r, rsy_s, rsy_r, rts_s, rts_r, rty_s, rty_r, gram_s, gram_r,
):
    n_z = n_rows // ROW_X
    me = lax.axis_index("rows")
    far = lax.axis_index("far")
    my_x, my_z = lax.rem(me, ROW_X), lax.div(me, ROW_X)
    my_y, my_c = lax.div(far, 2), lax.rem(far, 2)
    sib = my_y * 2 + 1 - my_c

    def ahead(k):
        return lax.rem(my_z + lax.div(k, ROW_X), n_z) * ROW_X + lax.rem(my_x + lax.rem(k, ROW_X), ROW_X)

    def behind(k):
        return lax.rem(my_z + n_z - lax.div(k, ROW_X), n_z) * ROW_X + lax.rem(my_x + ROW_X - lax.rem(k, ROW_X), ROW_X)

    def y_peer(d):
        return lax.rem(my_y + d, FAR_Y) * 2 + my_c

    def y_from(d):
        return lax.rem(my_y + FAR_Y - d, FAR_Y) * 2 + my_c

    def remote(src, dst, send, recv, rows, to_far):
        return pltpu.make_async_remote_copy(
            src_ref=src, dst_ref=dst, send_sem=send, recv_sem=recv,
            device_id={"rows": rows, "far": to_far}, device_id_type=MESH,
        )

    loads = [
        pltpu.make_async_copy(side_hbm, side, load_sem.at[0]),
        pltpu.make_async_copy(right_hbm, right_raw, load_sem.at[1]),
        pltpu.make_async_copy(left_hbm, left_raw, load_sem.at[2]),
        pltpu.make_async_copy(near_hbm, near_raw, load_sem.at[3]),
    ]
    for load in loads:
        load.start()

    barrier = pltpu.get_barrier_semaphore()

    def greet(k, carry):
        pl.semaphore_signal(barrier, inc=1, device_id={"rows": ahead(k), "far": far}, device_id_type=MESH)
        return carry

    lax.fori_loop(1, n_rows, greet, 0)
    for d in (1, 2, 3):
        pl.semaphore_signal(barrier, inc=1, device_id={"rows": me, "far": y_peer(d)}, device_id_type=MESH)
    pl.semaphore_signal(barrier, inc=1, device_id={"rows": me, "far": sib}, device_id_type=MESH)

    loads[0].wait()

    def put(q, slot, value):
        high, low = split(value)
        vcat[q, slot, :, :HALF] = high
        vcat[q, slot, :, HALF:] = low

    def take_side(o, carry):
        put(0, o + 8, side[o, :, :HALF])
        put(1, o + 8, side[o, :, HALF:])
        return carry

    lax.fori_loop(0, CL_DEV, take_side, 0)
    loads[1].wait()

    def take_right(t, carry):
        high, low = split(right_raw[t])
        right[t, :R, :] = high
        right[t, R:, :] = low
        return carry

    lax.fori_loop(0, n_rows, take_right, 0)
    pl.semaphore_wait(barrier, n_rows + 3)

    halo_to = lax.rem(me + n_rows - 1 + 2 * lax.div(far, 4), n_rows)

    def halo_copy(g):
        if g == 0:
            return remote(side_hbm.at[pl.ds(2 * far, 2)], halo_b.at[far], halo_s.at[0], halo_r.at[0], halo_to, far)
        return remote(own_u.at[g - 1, far], halo_u.at[g - 1, far], halo_s.at[g], halo_r.at[g], halo_to, far)

    halo_copy(0).start()

    def a2a(ap, q, k):
        return remote(coef_out.at[ap, q, k], coef_in.at[ap, q, k], a2a_s.at[ap, q, k], a2a_r.at[ap, q, k], ahead(k), far)

    def coefficient(q, t):
        return quadrants(jnp.dot(right[t], vcat[q, src_ref[t] + 8], preferred_element_type=F32))

    def send_coefficients(ap, q):
        def step(k, carry):
            coef_out[ap, q, k] = coefficient(q, ahead(k))
            a2a(ap, q, k).start()
            return carry

        lax.fori_loop(1, n_rows, step, 0)
        coef_in[ap, q, 0] = coefficient(q, me)

    send_coefficients(0, 0)
    send_coefficients(0, 1)

    def group_ref(g, who):
        if g == 0:
            return halo_b.at[who]
        if g <= 2:
            return own_u.at[g - 1, who]
        return halo_u.at[g - 3, who]

    def gather_y(g, d):
        ref = group_ref(g, far)
        return remote(ref, ref, agy_s.at[g, d], agy_r.at[g, d], me, y_peer(d))

    def gather_sib(g, d):
        ref = group_ref(g, y_from(d))
        return remote(ref, ref, ags_s.at[g, d], ags_r.at[g, d], me, sib)

    def gather_start(g):
        for d in (2, 1, 3):
            gather_y(g, d).start()
        gather_sib(g, 0).start()

    def gather_forward(g):
        for d in (1, 3, 2):
            ref = group_ref(g, y_from(d))
            remote(ref, ref, agy_s.at[g, d], agy_r.at[g, d], me, y_peer(d)).wait_recv()
            gather_sib(g, d).start()

    def gather_end(g):
        for d in range(FAR_Y):
            ref = group_ref(g, lax.rem(my_y + FAR_Y - d, FAR_Y) * 2 + 1 - my_c)
            remote(ref, ref, ags_s.at[g, d], ags_r.at[g, d], me, sib).wait_recv()

    halo_copy(0).wait_recv()
    gather_start(0)

    def tables(k, carry):
        mine = tgt_ref[behind(k)]
        found = n_rows
        for j in range(n_rows):
            same = jnp.logical_and(tgt_ref[behind(j)] == mine, j < k)
            found = jnp.where(same, j, found)
        prev[k] = found
        return carry

    lax.fori_loop(0, n_rows, tables, 0)

    def ends(o, carry):
        found = n_rows
        for j in range(n_rows):
            found = jnp.where(tgt_ref[behind(j)] == o, j, found)
        last[o] = found
        return carry

    lax.fori_loop(0, CL_DEV, ends, 0)
    chain[n_rows] = jnp.zeros((B, HALF), F32)
    loads[2].wait()

    def take_left(a, carry):
        high, low = split(left_raw[a].T)
        left[a, :B, :] = high
        left[a, B:, :] = low
        return carry

    lax.fori_loop(0, n_rows, take_left, 0)
    gather_forward(0)
    loads[3].wait()

    def take_near(o, carry):
        for s in range(NEAR_DEV):
            high, low = split(near_raw[o, s])
            near[o, :B, s * B : (s + 1) * B] = high
            near[o, B:, s * B : (s + 1) * B] = low
        return carry

    lax.fori_loop(0, CL_DEV, take_near, 0)
    gather_end(0)

    def take_halo_b(j, carry):
        who, i = lax.div(j, 2), lax.rem(j, 2)
        slot = lax.rem(j + 24, 32)
        put(0, slot, halo_b[who, i, :, :HALF])
        put(1, slot, halo_b[who, i, :, HALF:])
        return carry

    lax.fori_loop(0, CL_DEV, take_halo_b, 0)
    base = me * CL_DEV - 8

    def near_term(q):
        def step(o, carry):
            picked = [vcat[q, jnp.clip(cols_ref[s, o] - base, 0, 31)] for s in range(NEAR_DEV)]
            acc[q, o] = quadrants(jnp.dot(near[o], jnp.concatenate(picked, axis=0), preferred_element_type=F32))
            return carry

        lax.fori_loop(0, CL_DEV, step, 0)

    def far_term(ap, q, first, end):
        def step(k, carry):
            a2a_in = remote(coef_out.at[ap, q, k], coef_in.at[ap, q, k], a2a_s.at[ap, q, k], a2a_r.at[ap, q, k], ahead(k), far)
            a2a_in.wait_recv()
            add(ap, q, k)
            return carry

        def add(ap, q, k):
            both = jnp.concatenate(split(coef_in[ap, q, k]), axis=1)
            here = quadrants(jnp.dot(left[behind(k)], both, preferred_element_type=F32))
            chain[k] = here + chain[prev[k]]

        if first == 0:
            add(ap, q, 0)
        lax.fori_loop(max(first, 1), end, step, 0)

    near_term(0)
    near_term(1)
    far_term(0, 0, 0, n_rows)

    def finish_rows(q):
        def step(o, carry):
            part[q, lax.div(o, 4), lax.rem(lax.div(o, 2), 2), lax.rem(o, 2)] = acc[q, o] + chain[last[o]]
            return carry

        lax.fori_loop(0, CL_DEV, step, 0)

    def rows_sib(q):
        return remote(part.at[q, :, 1 - my_c], sib_in.at[q], rss_s.at[q], rss_r.at[q], me, sib)

    def rows_y(q, d):
        return remote(mix.at[q, d], y_in.at[q, d], rsy_s.at[q, d], rsy_r.at[q, d], me, y_peer(d))

    def rows_send(q):
        for d in (2, 1, 3):
            to_y = lax.rem(my_y + d, FAR_Y)
            mix[q, d] = part[q, to_y, my_c] + sib_in[q, to_y]
            rows_y(q, d).start()

    def rows_own(q):
        for d in (1, 2, 3):
            rows_y(q, d).wait_recv()
        own_u[q, far] = (part[q, my_y, my_c] + sib_in[q, my_y]) + (y_in[q, 1] + y_in[q, 2] + y_in[q, 3])

    def take_own(q):
        def step(j, carry):
            put(q, j + 8, own_u[q, lax.div(j, 2), lax.rem(j, 2)])
            return carry

        lax.fori_loop(0, CL_DEV, step, 0)

    def take_halo(q):
        def step(j, carry):
            put(q, lax.rem(j + 24, 32), halo_u[q, lax.div(j, 2), lax.rem(j, 2)])
            return carry

        lax.fori_loop(0, CL_DEV, step, 0)

    def halo_pass(q):
        halo_copy(q + 1).wait_recv()
        gather_start(q + 3)

    quarter = n_rows // 4
    finish_rows(0)
    rows_sib(0).start()
    far_term(0, 1, 0, quarter)
    rows_sib(0).wait_recv()
    rows_send(0)
    far_term(0, 1, quarter, 2 * quarter)
    rows_own(0)
    halo_copy(1).start()
    gather_start(1)
    far_term(0, 1, 2 * quarter, 3 * quarter)
    gather_forward(1)
    gather_end(1)
    take_own(0)
    send_coefficients(1, 0)
    halo_pass(0)

    far_term(0, 1, 3 * quarter, n_rows)
    finish_rows(1)
    rows_sib(1).start()
    gather_forward(3)
    rows_sib(1).wait_recv()
    rows_send(1)
    gather_end(3)
    take_halo(0)
    near_term(0)
    rows_own(1)
    halo_copy(2).start()
    gather_start(2)
    far_term(1, 0, 0, quarter)
    gather_forward(2)
    gather_end(2)
    take_own(1)
    send_coefficients(1, 1)
    halo_pass(1)

    def finish_columns(q):
        def step(o, carry):
            tile = (acc[q, o] + chain[last[o]]).T
            lanes = pl.ds(pl.multiple_of(o * B, B), B)
            for j in range(4):
                part_t[q, j // 2, j % 2, :, lanes] = tile[32 * j : 32 * j + 32]
            return carry

        lax.fori_loop(0, CL_DEV, step, 0)

    def columns_sib(q):
        return remote(part_t.at[q, :, 1 - my_c], sib_t.at[q], rts_s.at[q], rts_r.at[q], me, sib)

    def columns_y(q, j):
        to_y = 2 * q + j
        d = lax.rem(to_y + FAR_Y - my_y, FAR_Y)
        return remote(mix_t.at[q, j], y_t.at[d], rty_s.at[q, j], rty_r.at[d], me, to_y * 2 + my_c)

    def columns_send(q):
        for j in range(2):
            @pl.when(my_y != 2 * q + j)
            def _():
                mix_t[q, j] = part_t[q, j, my_c] + sib_t[q, j]
                columns_y(q, j).start()

    def columns_own(q):
        for j in range(2):
            @pl.when(my_y == 2 * q + j)
            def _():
                for d in (1, 2, 3):
                    remote(mix_t.at[q, j], y_t.at[d], rty_s.at[q, j], rty_r.at[d], me, y_peer(d)).wait_recv()
                own_w[...] = (part_t[q, j, my_c] + sib_t[q, j]) + (y_t[1] + y_t[2] + y_t[3])

    far_term(1, 0, quarter, n_rows)
    finish_columns(0)
    columns_sib(0).start()
    gather_forward(4)
    columns_sib(0).wait_recv()
    columns_send(0)
    gather_end(4)
    take_halo(1)
    near_term(1)
    my_half = lax.div(my_y, 2)

    def turn(o, carry):
        lanes = pl.ds(pl.multiple_of(o * B, B), B)
        turned[0, :, lanes] = side[o, :, pl.ds(pl.multiple_of(my_half * HALF, HALF), HALF)].T
        turned[1, :, lanes] = own_u[my_half, lax.div(o, 2), lax.rem(o, 2)].T
        return carry

    lax.fori_loop(0, CL_DEV, turn, 0)
    columns_own(0)
    far_term(1, 1, 0, n_rows)
    finish_columns(1)
    columns_sib(1).start()
    columns_sib(1).wait_recv()
    columns_send(1)
    columns_own(1)

    mine = pl.ds(pl.multiple_of(lax.rem(far, 4) * 32, 32), 32)
    lane = lax.broadcasted_iota(jnp.int32, (32, B), 1)

    def dots(o, sums):
        lanes = pl.ds(pl.multiple_of(o * B, B), B)
        b, u, w = turned[0, mine, lanes], turned[1, mine, lanes], own_w[:, lanes]
        return tuple(total + item for total, item in zip(sums, (b * b, b * u, u * u, b * w, u * w, w * w)))

    sums = lax.fori_loop(0, CL_DEV, dots, tuple(jnp.zeros((32, B), F32) for _ in range(6)))
    table = jnp.zeros((32, B), F32)
    for j in range(6):
        table = jnp.where(lane == j, jnp.sum(sums[j], axis=1, keepdims=True), table)
    flat = jnp.concatenate([table, jnp.zeros((B - 32, B), F32)], axis=0).T[:8]
    gram_out[...] = flat

    def gram(k):
        return remote(gram_out, gram_in.at[k], gram_s.at[k], gram_r.at[k], ahead(k), far)

    def gram_start(k, carry):
        gram(k).start()
        return carry

    lax.fori_loop(1, n_rows, gram_start, 0)
    gram_in[0] = flat

    def gram_add(k, total):
        gram(k).wait_recv()
        return total + gram_in[k]

    total = lax.fori_loop(1, n_rows, gram_add, gram_in[0])
    weights = combine([total[j : j + 1] for j in range(6)])
    stack = jnp.concatenate(list(weights) + [jnp.zeros((B - 5, B), F32)], axis=0).T
    parts = [stack[:32, j : j + 1] for j in range(5)]
    b, u, w = turned[0, mine, :], turned[1, mine, :], own_w[...]
    sol_ref[...] = parts[0] * b + parts[1] * u
    res_ref[...] = parts[2] * b + parts[3] * u + parts[4] * w

    def settle(k, carry):
        for ap in range(2):
            for q in range(2):
                a2a(ap, q, k).wait_send()
        gram(k).wait_send()
        return carry

    lax.fori_loop(1, n_rows, settle, 0)
    for g in range(3):
        halo_copy(g).wait_send()
    for g in range(5):
        for d in range(FAR_Y):
            if d > 0:
                gather_y(g, d).wait_send()
            gather_sib(g, d).wait_send()
    for q in range(2):
        rows_sib(q).wait_send()
        columns_sib(q).wait_send()
        for d in (1, 2, 3):
            rows_y(q, d).wait_send()
        for j in range(2):
            @pl.when(my_y != 2 * q + j)
            def _():
                columns_y(q, j).wait_send()


def solution(mesh):
    n_rows = mesh.shape["rows"]
    dma = pltpu.SemaphoreType.DMA

    def shards(right_side, near_blocks, near_cols, far_src, far_tgt, far_left, far_right):
        anywhere = pl.BlockSpec(memory_space=pl.ANY)
        scalars = pl.BlockSpec(memory_space=pltpu.SMEM)
        vector = pl.BlockSpec(memory_space=pltpu.VMEM)
        sol, res = pl.pallas_call(
            functools.partial(kernel, n_rows),
            out_shape=(jax.ShapeDtypeStruct((32, CL_DEV * B), F32),) * 2,
            in_specs=[scalars] * 3 + [anywhere] * 4,
            out_specs=(vector, vector),
            scratch_shapes=[
                pltpu.VMEM((CL_DEV, B, 2 * HALF), F32),
                pltpu.VMEM((CL_DEV, NEAR_DEV, B, B), F32),
                pltpu.VMEM((CL_DEV, 2 * B, NEAR_DEV * B), BF16),
                pltpu.VMEM((n_rows, R, B), F32),
                pltpu.VMEM((n_rows, 2 * B, R), BF16),
                pltpu.VMEM((n_rows, R, B), F32),
                pltpu.VMEM((n_rows, 2 * R, B), BF16),
                pltpu.VMEM((2, 32, B, 2 * HALF), BF16),
                pltpu.VMEM((2, 2, n_rows, R, HALF), F32),
                pltpu.VMEM((2, 2, n_rows, R, HALF), F32),
                pltpu.VMEM((8, 2, B, 2 * HALF), F32),
                pltpu.VMEM((2, 8, 2, B, HALF), F32),
                pltpu.VMEM((2, 8, 2, B, HALF), F32),
                pltpu.VMEM((2, CL_DEV, B, HALF), F32),
                pltpu.VMEM((n_rows + 1, B, HALF), F32),
                pltpu.VMEM((2, 4, 2, 2, B, HALF), F32),
                pltpu.VMEM((2, 2, 2, 32, CL_DEV * B), F32),
                pltpu.VMEM((2, 4, 2, B, HALF), F32),
                pltpu.VMEM((2, 4, 2, B, HALF), F32),
                pltpu.VMEM((2, 4, 2, B, HALF), F32),
                pltpu.VMEM((2, 2, 32, CL_DEV * B), F32),
                pltpu.VMEM((2, 2, 32, CL_DEV * B), F32),
                pltpu.VMEM((4, 32, CL_DEV * B), F32),
                pltpu.VMEM((2, HALF, CL_DEV * B), F32),
                pltpu.VMEM((32, CL_DEV * B), F32),
                pltpu.VMEM((8, B), F32),
                pltpu.VMEM((n_rows, 8, B), F32),
                pltpu.SMEM((n_rows,), jnp.int32),
                pltpu.SMEM((CL_DEV,), jnp.int32),
                dma((4,)), dma((2, 2, n_rows)), dma((2, 2, n_rows)), dma((3,)), dma((3,)),
                dma((5, 4)), dma((5, 4)), dma((5, 4)), dma((5, 4)),
                dma((2,)), dma((2,)), dma((2, 4)), dma((2, 4)),
                dma((2,)), dma((2,)), dma((2, 2)), dma((4,)),
                dma((n_rows,)), dma((n_rows,)),
            ],
            compiler_params=pltpu.CompilerParams(collective_id=0, has_side_effects=True, vmem_limit_bytes=60 << 20),
            name="gmres",
        )(
            near_cols.T,
            far_src.reshape(n_rows),
            far_tgt.reshape(n_rows),
            right_side.reshape(CL_DEV, B, 2 * HALF),
            near_blocks,
            jnp.swapaxes(far_left.reshape(n_rows, B, R), 1, 2),
            jnp.swapaxes(far_right.reshape(n_rows, B, R), 1, 2),
        )
        return sol.T, res.T

    return jax.shard_map(
        shards,
        mesh=mesh,
        in_specs=(
            P("rows", None),
            P("rows", "far", None, None),
            P("rows", "far"),
            P("rows", None, "far"),
            P("rows", None, "far"),
            P("rows", None, "far", None, None),
            P("rows", None, "far", None, None),
        ),
        out_specs=(P("rows", "far"), P("rows", "far")),
        check_vma=False,
    )
```

time: 509 us -> 165 us (0.32); the launches traced: 503 us -> 165 us
  waiting for transfers between devices: 221 us -> 0 us
  Pallas kernels: 0 us -> 161 us
  matrix products: 84 us -> 0 us
  blocking collectives: 75 us -> 0 us
  local copies, waits for them, and re-layouts: 62.4 us -> 3.34 us
  starting transfers between devices: 34.8 us -> 0 us
  between operations: 14.4 us -> 0.64 us
  other arithmetic: 10.8 us -> 0 us
    pallas_call x0 -> x1, Pallas kernels: none -> 161 us  [shards(): pl.pallas_call(functools.partial(kernel, n_rows), out_shape=(jax.ShapeDty...]
    psum x1 -> x0, waiting for transfers between devices: 89.9 us -> none  [shards(): image_one = lax.psum(partial_image(right_side), 'far')]
    dot_general x8 -> x0, matrix products: 84 us -> none  [the longest x2 43.2 us: near_term(): jnp.einsum('cspq,csqn->cpn', near_blocks, picked, precision=TOP_PRECISION)]
    ppermute x4 -> x0, waiting for transfers between devices: 80.3 us -> none  [the longest x2 80.3 us: with_halo(): lax.ppermute(head, axis, [((i + 1) % count, i) for i in range(ends)])]
    psum x1 -> x0, blocking collectives: 75 us -> none  [shards(): lax.psum(jnp.stack([column_dots(left, right) for left, right in pairs]),...]
    reduce_scatter x1 -> x0, waiting for transfers between devices: 51.1 us -> none  [shards(): lax.psum_scatter(partial_image(image_one), 'far', scatter_dimension=1, ti...]
    gather x4 -> x0, local copies, waits for them, and re-layouts: 30.5 us -> none  [the longest x2 21.8 us: near_term(): picked = jnp.take(clusters, near_cols - offset, axis=0)]
    all_to_all x2 -> x0, starting transfers between devices: 21.5 us -> none  [far_term(): lax.all_to_all(coefficients, 'rows', split_axis=0, concat_axis=0, tiled=T...]
  transfers between devices with their start and end apart: 8 -> 0, of which waited for: 4 -> 0; matrix products, arithmetic and copies ran while one was open for 8% -> 0% of each run, Pallas kernels for 0% -> 0%
where the time goes in v2:
time: 165 us
  Pallas kernels  161 us (98%)
  local copies, waits for them, and re-layouts  3.34 us (2%)
    pallas_call x1, Pallas kernels, shards(): pl.pallas_call(functools.partial(kernel, n_rows), out_shape=(jax.ShapeDty...  161 us
    unnamed x2, local copies, waits for them, and re-layouts  3.34 us

profile of v2, /device:TPU:24, one launch (start us, length us, event | category | flops | bytes accessed | tf_op | source)
XLA Modules:
  0.0 165.3 jit_solution(10530362832564919737)
XLA Ops:
  0.6 161.3 %gmres.1 = (f32[32,2048]{1,0:T(8,128)}, f32[32,2048]{1,0:T(8,128)}) custom-call(s32[6,16]{1,0:T(8,128)} %bitcast.17, s32[32]{0:T(128)} %bitcast.18, s32[32]{0:T(128)} %bitcast.19, f32[16,128,256]{2,1,0:T(8,128)} %bitcast.12, f32[16,6,128,128]{3,2,1,0:T(8,128)} %near_hbm.1, f32[32,64,128]{2,1,0:T(8,128)} %bitcast.13, f32[32,64,128]{2,1,0:T(8,128)} %bitcast.14), custom_call_target="tpu_custom_call" | custom-call | tf_op jit(solution)/shard_map/gmres/pallas_call | solution.py:500
  161.9 1.7 %copy.11 = f32[2048,32]{0,1:T(8,128)} copy(f32[2048,32]{0,1:T(8,128)} %bitcast.16) | data formatting | bytes 524288
  163.6 1.7 %copy.12 = f32[2048,32]{0,1:T(8,128)} copy(f32[2048,32]{0,1:T(8,128)} %bitcast.15) | data formatting | bytes 524288

commit v3 on v2

--- a/solution.py
+++ b/solution.py
@@ -14,6 +14,8 @@
 CL_DEV = 16
 ROW_X = 4
 FAR_Y = 4
+UNROLL = 8
+ROW_HALF = 1024
 EPS = 1e-06
 MESH = pl.DeviceIdType.MESH
 F32 = jnp.float32
@@ -28,6 +30,12 @@
 def quadrants(value):
     rows = value.shape[0] // 2
     return (value[:rows, :HALF] + value[:rows, HALF:]) + (value[rows:, :HALF] + value[rows:, HALF:])
+
+
+def interleave(value):
+    lane = lax.broadcasted_iota(jnp.int32, (value.shape[0], HALF), 1)
+    first, second = value[:, :HALF], value[:, HALF:]
+    return jnp.where(lane < 64, first, pltpu.roll(second, 64, 1)), jnp.where(lane < 64, pltpu.roll(first, 64, 1), second)
 
 
 def combine(gram):
@@ -132,8 +140,9 @@
         vcat[q, slot, :, HALF:] = low
 
     def take_side(o, carry):
-        put(0, o + 8, side[o, :, :HALF])
-        put(1, o + 8, side[o, :, HALF:])
+        for q, item in enumerate(interleave(side[o])):
+            put(q, o + 8, item)
+            side[o, :, q * HALF : (q + 1) * HALF] = item
         return carry
 
     lax.fori_loop(0, CL_DEV, take_side, 0)
@@ -164,13 +173,17 @@
         return quadrants(jnp.dot(right[t], vcat[q, src_ref[t] + 8], preferred_element_type=F32))
 
     def send_coefficients(ap, q):
-        def step(k, carry):
+        def step(g, carry):
+            for k in [g * UNROLL + j for j in range(UNROLL)]:
+                coef_out[ap, q, k] = coefficient(q, ahead(k))
+                a2a(ap, q, k).start()
+            return carry
+
+        lax.fori_loop(1, n_rows // UNROLL, step, 0)
+        coef_in[ap, q, 0] = coefficient(q, me)
+        for k in range(1, UNROLL):
             coef_out[ap, q, k] = coefficient(q, ahead(k))
             a2a(ap, q, k).start()
-            return carry
-
-        lax.fori_loop(1, n_rows, step, 0)
-        coef_in[ap, q, 0] = coefficient(q, me)
 
     send_coefficients(0, 0)
     send_coefficients(0, 1)
@@ -254,39 +267,43 @@
     def take_halo_b(j, carry):
         who, i = lax.div(j, 2), lax.rem(j, 2)
         slot = lax.rem(j + 24, 32)
-        put(0, slot, halo_b[who, i, :, :HALF])
-        put(1, slot, halo_b[who, i, :, HALF:])
+        for q, item in enumerate(interleave(halo_b[who, i])):
+            put(q, slot, item)
         return carry
 
     lax.fori_loop(0, CL_DEV, take_halo_b, 0)
     base = me * CL_DEV - 8
 
     def near_term(q):
-        def step(o, carry):
-            picked = [vcat[q, jnp.clip(cols_ref[s, o] - base, 0, 31)] for s in range(NEAR_DEV)]
-            acc[q, o] = quadrants(jnp.dot(near[o], jnp.concatenate(picked, axis=0), preferred_element_type=F32))
+        def step(g, carry):
+            for o in [g * 4 + j for j in range(4)]:
+                picked = [vcat[q, jnp.clip(cols_ref[s, o] - base, 0, 31)] for s in range(NEAR_DEV)]
+                acc[q, o] = quadrants(jnp.dot(near[o], jnp.concatenate(picked, axis=0), preferred_element_type=F32))
             return carry
 
-        lax.fori_loop(0, CL_DEV, step, 0)
+        lax.fori_loop(0, CL_DEV // 4, step, 0)
 
     def far_term(ap, q, first, end):
-        def step(k, carry):
-            a2a_in = remote(coef_out.at[ap, q, k], coef_in.at[ap, q, k], a2a_s.at[ap, q, k], a2a_r.at[ap, q, k], ahead(k), far)
-            a2a_in.wait_recv()
-            add(ap, q, k)
+        def step(g, carry):
+            several(g)
             return carry
 
-        def add(ap, q, k):
-            both = jnp.concatenate(split(coef_in[ap, q, k]), axis=1)
-            here = quadrants(jnp.dot(left[behind(k)], both, preferred_element_type=F32))
-            chain[k] = here + chain[prev[k]]
+        def several(g, skip=0):
+            ks = [g * UNROLL + j for j in range(UNROLL)]
+            for k in ks[skip:]:
+                a2a(ap, q, k).wait_recv()
+            here = []
+            for k in ks:
+                both = jnp.concatenate(split(coef_in[ap, q, k]), axis=1)
+                here.append(quadrants(jnp.dot(left[behind(k)], both, preferred_element_type=F32)))
+            for k, item in zip(ks, here):
+                chain[k] = item + chain[prev[k]]
 
         if first == 0:
-            add(ap, q, 0)
-        lax.fori_loop(max(first, 1), end, step, 0)
+            several(0, 1)
+        lax.fori_loop(max(first // UNROLL, 1), end // UNROLL, step, 0)
 
     near_term(0)
-    near_term(1)
     far_term(0, 0, 0, n_rows)
 
     def finish_rows(q):
@@ -296,22 +313,28 @@
 
         lax.fori_loop(0, CL_DEV, step, 0)
 
-    def rows_sib(q):
-        return remote(part.at[q, :, 1 - my_c], sib_in.at[q], rss_s.at[q], rss_r.at[q], me, sib)
+    def rows_sib(q, d):
+        to_y = lax.rem(my_y + d, FAR_Y)
+        return remote(part.at[q, to_y, 1 - my_c], sib_in.at[q, d], rss_s.at[q, d], rss_r.at[q, d], me, sib)
 
     def rows_y(q, d):
         return remote(mix.at[q, d], y_in.at[q, d], rsy_s.at[q, d], rsy_r.at[q, d], me, y_peer(d))
 
+    def rows_start(q):
+        for d in (2, 1, 3, 0):
+            rows_sib(q, d).start()
+
     def rows_send(q):
         for d in (2, 1, 3):
-            to_y = lax.rem(my_y + d, FAR_Y)
-            mix[q, d] = part[q, to_y, my_c] + sib_in[q, to_y]
+            rows_sib(q, d).wait_recv()
+            mix[q, d] = part[q, lax.rem(my_y + d, FAR_Y), my_c] + sib_in[q, d]
             rows_y(q, d).start()
+        rows_sib(q, 0).wait_recv()
 
     def rows_own(q):
         for d in (1, 2, 3):
             rows_y(q, d).wait_recv()
-        own_u[q, far] = (part[q, my_y, my_c] + sib_in[q, my_y]) + (y_in[q, 1] + y_in[q, 2] + y_in[q, 3])
+        own_u[q, far] = (part[q, my_y, my_c] + sib_in[q, 0]) + (y_in[q, 1] + y_in[q, 2] + y_in[q, 3])
 
     def take_own(q):
         def step(j, carry):
@@ -331,85 +354,84 @@
         halo_copy(q + 1).wait_recv()
         gather_start(q + 3)
 
-    quarter = n_rows // 4
     finish_rows(0)
-    rows_sib(0).start()
-    far_term(0, 1, 0, quarter)
-    rows_sib(0).wait_recv()
+    rows_start(0)
+    near_term(1)
     rows_send(0)
-    far_term(0, 1, quarter, 2 * quarter)
     rows_own(0)
     halo_copy(1).start()
     gather_start(1)
-    far_term(0, 1, 2 * quarter, 3 * quarter)
     gather_forward(1)
     gather_end(1)
     take_own(0)
     send_coefficients(1, 0)
     halo_pass(0)
 
-    far_term(0, 1, 3 * quarter, n_rows)
+    far_term(0, 1, 0, n_rows)
     finish_rows(1)
-    rows_sib(1).start()
+    rows_start(1)
+    rows_send(1)
     gather_forward(3)
-    rows_sib(1).wait_recv()
-    rows_send(1)
-    gather_end(3)
-    take_halo(0)
-    near_term(0)
     rows_own(1)
     halo_copy(2).start()
     gather_start(2)
-    far_term(1, 0, 0, quarter)
     gather_forward(2)
     gather_end(2)
     take_own(1)
     send_coefficients(1, 1)
+    gather_end(3)
+    take_halo(0)
+    near_term(0)
     halo_pass(1)
 
-    def finish_columns(q):
-        def step(o, carry):
-            tile = (acc[q, o] + chain[last[o]]).T
-            lanes = pl.ds(pl.multiple_of(o * B, B), B)
-            for j in range(4):
-                part_t[q, j // 2, j % 2, :, lanes] = tile[32 * j : 32 * j + 32]
+    def finish_columns(q, h):
+        def step(g, carry):
+            for o in [h * 8 + g * 4 + j for j in range(4)]:
+                tile = (acc[q, o] + chain[last[o]]).T
+                lanes = pl.ds(pl.multiple_of((g * 4 + o % 4) * B, B), B)
+                for j in range(4):
+                    part_t[q, h, j // 2, j % 2, :, lanes] = tile[32 * j : 32 * j + 32]
             return carry
 
-        lax.fori_loop(0, CL_DEV, step, 0)
-
-    def columns_sib(q):
-        return remote(part_t.at[q, :, 1 - my_c], sib_t.at[q], rts_s.at[q], rts_r.at[q], me, sib)
-
-    def columns_y(q, j):
-        to_y = 2 * q + j
+        for g in range(2):
+            step(g, 0)
+
+    def columns_sib(q, h):
+        return remote(part_t.at[q, h, :, 1 - my_c], sib_t.at[q, h], rts_s.at[q, h], rts_r.at[q, h], me, sib)
+
+    def columns_y(q, h, j):
+        to_y = q + 2 * j
         d = lax.rem(to_y + FAR_Y - my_y, FAR_Y)
-        return remote(mix_t.at[q, j], y_t.at[d], rty_s.at[q, j], rty_r.at[d], me, to_y * 2 + my_c)
-
-    def columns_send(q):
+        return remote(mix_t.at[q, h, j], y_t.at[h, d], rty_s.at[q, h, j], rty_r.at[h, d], me, to_y * 2 + my_c)
+
+    def columns_send(q, h):
         for j in range(2):
-            @pl.when(my_y != 2 * q + j)
+            @pl.when(my_y != q + 2 * j)
             def _():
-                mix_t[q, j] = part_t[q, j, my_c] + sib_t[q, j]
-                columns_y(q, j).start()
-
-    def columns_own(q):
+                mix_t[q, h, j] = part_t[q, h, j, my_c] + sib_t[q, h, j]
+                columns_y(q, h, j).start()
+
+    def columns_own(q, h):
         for j in range(2):
-            @pl.when(my_y == 2 * q + j)
+            @pl.when(my_y == q + 2 * j)
             def _():
                 for d in (1, 2, 3):
-                    remote(mix_t.at[q, j], y_t.at[d], rty_s.at[q, j], rty_r.at[d], me, y_peer(d)).wait_recv()
-                own_w[...] = (part_t[q, j, my_c] + sib_t[q, j]) + (y_t[1] + y_t[2] + y_t[3])
-
-    far_term(1, 0, quarter, n_rows)
-    finish_columns(0)
-    columns_sib(0).start()
+                    remote(mix_t.at[q, h, j], y_t.at[h, d], rty_s.at[q, h, j], rty_r.at[h, d], me, y_peer(d)).wait_recv()
+                mine = (part_t[q, h, j, my_c] + sib_t[q, h, j]) + (y_t[h, 1] + y_t[h, 2] + y_t[h, 3])
+                own_w[:, h * ROW_HALF : (h + 1) * ROW_HALF] = mine
+
+    far_term(1, 0, 0, n_rows)
+    for h in range(2):
+        finish_columns(0, h)
+        columns_sib(0, h).start()
     gather_forward(4)
-    columns_sib(0).wait_recv()
-    columns_send(0)
+    for h in range(2):
+        columns_sib(0, h).wait_recv()
+        columns_send(0, h)
     gather_end(4)
     take_halo(1)
     near_term(1)
-    my_half = lax.div(my_y, 2)
+    my_half = lax.rem(my_y, 2)
 
     def turn(o, carry):
         lanes = pl.ds(pl.multiple_of(o * B, B), B)
@@ -418,15 +440,19 @@
         return carry
 
     lax.fori_loop(0, CL_DEV, turn, 0)
-    columns_own(0)
+    for h in range(2):
+        columns_own(0, h)
     far_term(1, 1, 0, n_rows)
-    finish_columns(1)
-    columns_sib(1).start()
-    columns_sib(1).wait_recv()
-    columns_send(1)
-    columns_own(1)
-
-    mine = pl.ds(pl.multiple_of(lax.rem(far, 4) * 32, 32), 32)
+    for h in range(2):
+        finish_columns(1, h)
+        columns_sib(1, h).start()
+    for h in range(2):
+        columns_sib(1, h).wait_recv()
+        columns_send(1, h)
+    for h in range(2):
+        columns_own(1, h)
+
+    mine = pl.ds(pl.multiple_of((lax.div(my_y, 2) * 2 + my_c) * 32, 32), 32)
     lane = lax.broadcasted_iota(jnp.int32, (32, B), 1)
 
     def dots(o, sums):
@@ -479,14 +505,24 @@
                 gather_y(g, d).wait_send()
             gather_sib(g, d).wait_send()
     for q in range(2):
-        rows_sib(q).wait_send()
-        columns_sib(q).wait_send()
+        for d in range(FAR_Y):
+            rows_sib(q, d).wait_send()
         for d in (1, 2, 3):
             rows_y(q, d).wait_send()
-        for j in range(2):
-            @pl.when(my_y != 2 * q + j)
-            def _():
-                columns_y(q, j).wait_send()
+        for h in range(2):
+            columns_sib(q, h).wait_send()
+            for j in range(2):
+                @pl.when(my_y != q + 2 * j)
+                def _():
+                    columns_y(q, h, j).wait_send()
+
+
+def deliver(sol_in, res_in, sol_out, res_out, sem):
+    copies = [pltpu.make_async_copy(sol_in, sol_out, sem.at[0]), pltpu.make_async_copy(res_in, res_out, sem.at[1])]
+    for copy in copies:
+        copy.start()
+    for copy in copies:
+        copy.wait()
 
 
 def solution(mesh):
@@ -519,13 +555,13 @@
                 pltpu.VMEM((2, CL_DEV, B, HALF), F32),
                 pltpu.VMEM((n_rows + 1, B, HALF), F32),
                 pltpu.VMEM((2, 4, 2, 2, B, HALF), F32),
-                pltpu.VMEM((2, 2, 2, 32, CL_DEV * B), F32),
+                pltpu.VMEM((2, 2, 2, 2, 32, ROW_HALF), F32),
                 pltpu.VMEM((2, 4, 2, B, HALF), F32),
                 pltpu.VMEM((2, 4, 2, B, HALF), F32),
                 pltpu.VMEM((2, 4, 2, B, HALF), F32),
-                pltpu.VMEM((2, 2, 32, CL_DEV * B), F32),
-                pltpu.VMEM((2, 2, 32, CL_DEV * B), F32),
-                pltpu.VMEM((4, 32, CL_DEV * B), F32),
+                pltpu.VMEM((2, 2, 2, 32, ROW_HALF), F32),
+                pltpu.VMEM((2, 2, 2, 32, ROW_HALF), F32),
+                pltpu.VMEM((2, 4, 32, ROW_HALF), F32),
                 pltpu.VMEM((2, HALF, CL_DEV * B), F32),
                 pltpu.VMEM((32, CL_DEV * B), F32),
                 pltpu.VMEM((8, B), F32),
@@ -534,8 +570,8 @@
                 pltpu.SMEM((CL_DEV,), jnp.int32),
                 dma((4,)), dma((2, 2, n_rows)), dma((2, 2, n_rows)), dma((3,)), dma((3,)),
                 dma((5, 4)), dma((5, 4)), dma((5, 4)), dma((5, 4)),
-                dma((2,)), dma((2,)), dma((2, 4)), dma((2, 4)),
-                dma((2,)), dma((2,)), dma((2, 2)), dma((4,)),
+                dma((2, 4)), dma((2, 4)), dma((2, 4)), dma((2, 4)),
+                dma((2, 2)), dma((2, 2)), dma((2, 2, 2)), dma((2, 4)),
                 dma((n_rows,)), dma((n_rows,)),
             ],
             compiler_params=pltpu.CompilerParams(collective_id=0, has_side_effects=True, vmem_limit_bytes=60 << 20),
@@ -549,6 +585,14 @@
             jnp.swapaxes(far_left.reshape(n_rows, B, R), 1, 2),
             jnp.swapaxes(far_right.reshape(n_rows, B, R), 1, 2),
         )
+        sol, res = pl.pallas_call(
+            deliver,
+            out_shape=(jax.ShapeDtypeStruct((32, CL_DEV * B), F32),) * 2,
+            in_specs=[anywhere] * 2,
+            out_specs=(anywhere, anywhere),
+            scratch_shapes=[dma((2,))],
+            name="deliver",
+        )(sol, res)
         return sol.T, res.T
 
     return jax.shard_map(

time: 165 us -> 168 us (1.018)
  Pallas kernels: 161 us -> 167 us
  local copies, waits for them, and re-layouts: 3.34 us -> 0 us
    pallas_call x0 -> x1, Pallas kernels: none -> 17 us  [shards(): pl.pallas_call(deliver, out_shape=(jax.ShapeDtypeStruct((32, CL_DEV * B),...]
    pallas_call x1, Pallas kernels: 161 us -> 150 us  [shards(): pl.pallas_call(functools.partial(kernel, n_rows), out_shape=(jax.ShapeDty...]
    unnamed x2 -> x0, local copies, waits for them, and re-layouts: 3.34 us -> none
where the time goes in v3:
time: 168 us
  Pallas kernels  167 us (99%)
    pallas_call x1, Pallas kernels, shards(): pl.pallas_call(functools.partial(kernel, n_rows), out_shape=(jax.ShapeDty...  150 us
    pallas_call x1, Pallas kernels, shards(): pl.pallas_call(deliver, out_shape=(jax.ShapeDtypeStruct((32, CL_DEV * B),...  17 us

profile of v3, /device:TPU:24, one launch (start us, length us, event | category | flops | bytes accessed | tf_op | source)
XLA Modules:
  0.0 167.5 jit_solution(13077983179236755626)
XLA Ops:
  0.6 149.9 %gmres.1 = (f32[32,2048]{1,0:T(8,128)}, f32[32,2048]{1,0:T(8,128)}) custom-call(s32[6,16]{1,0:T(8,128)} %bitcast.15, s32[32]{0:T(128)} %bitcast.16, s32[32]{0:T(128)} %bitcast.17, f32[16,128,256]{2,1,0:T(8,128)} %bitcast.12, f32[16,6,128,128]{3,2,1,0:T(8,128)} %near_hbm.1, f32[32,64,128]{2,1,0:T(8,128)} %bitcast.13, f32[32,64,128]{2,1,0:T(8,128)} %bitcast.14), custom_call_target="tpu_custom_call" | custom-call | tf_op jit(solution)/shard_map/gmres/pallas_call | solution.py:536
  150.5 17.0 %deliver.1 = (f32[32,2048]{1,0:T(8,128)}, f32[32,2048]{1,0:T(8,128)}) custom-call(f32[32,2048]{1,0:T(8,128)} %get-tuple-element.6.sol_in, f32[32,2048]{1,0:T(8,128)} %get-tuple-element.7.res_in), custom_call_target="tpu_custom_call" | custom-call | tf_op jit(solution)/shard_map/deliver/pallas_call | solution.py:588

commit v4 on v3

--- a/solution.py
+++ b/solution.py
@@ -160,14 +160,20 @@
     halo_to = lax.rem(me + n_rows - 1 + 2 * lax.div(far, 4), n_rows)
 
     def halo_copy(g):
-        if g == 0:
-            return remote(side_hbm.at[pl.ds(2 * far, 2)], halo_b.at[far], halo_s.at[0], halo_r.at[0], halo_to, far)
+        if g >= 3:
+            rows = side.at[pl.ds(2 * far, 2), :, pl.ds((g - 3) * HALF, HALF)]
+            return remote(rows, halo_b.at[g - 3, far], halo_s.at[g], halo_r.at[g], halo_to, far)
         return remote(own_u.at[g - 1, far], halo_u.at[g - 1, far], halo_s.at[g], halo_r.at[g], halo_to, far)
 
-    halo_copy(0).start()
+    halo_copy(3).start()
+    halo_copy(4).start()
 
     def a2a(ap, q, k):
         return remote(coef_out.at[ap, q, k], coef_in.at[ap, q, k], a2a_s.at[ap, q, k], a2a_r.at[ap, q, k], ahead(k), far)
+
+    def settle(ap, q, k):
+        a2a(ap, q, k).wait_send()
+        return 0
 
     def coefficient(q, t):
         return quadrants(jnp.dot(right[t], vcat[q, src_ref[t] + 8], preferred_element_type=F32))
@@ -189,8 +195,8 @@
     send_coefficients(0, 1)
 
     def group_ref(g, who):
-        if g == 0:
-            return halo_b.at[who]
+        if g in (0, 5):
+            return halo_b.at[g // 5, who]
         if g <= 2:
             return own_u.at[g - 1, who]
         return halo_u.at[g - 3, who]
@@ -219,8 +225,9 @@
             ref = group_ref(g, lax.rem(my_y + FAR_Y - d, FAR_Y) * 2 + 1 - my_c)
             remote(ref, ref, ags_s.at[g, d], ags_r.at[g, d], me, sib).wait_recv()
 
-    halo_copy(0).wait_recv()
-    gather_start(0)
+    for q in range(2):
+        halo_copy(q + 3).wait_recv()
+        gather_start(q * 5)
 
     def tables(k, carry):
         mine = tgt_ref[behind(k)]
@@ -262,16 +269,16 @@
         return carry
 
     lax.fori_loop(0, CL_DEV, take_near, 0)
+
+    def take_halo(q, halo):
+        def step(j, carry):
+            put(q, lax.rem(j + 24, 32), halo[q, lax.div(j, 2), lax.rem(j, 2)])
+            return carry
+
+        lax.fori_loop(0, CL_DEV, step, 0)
+
     gather_end(0)
-
-    def take_halo_b(j, carry):
-        who, i = lax.div(j, 2), lax.rem(j, 2)
-        slot = lax.rem(j + 24, 32)
-        for q, item in enumerate(interleave(halo_b[who, i])):
-            put(q, slot, item)
-        return carry
-
-    lax.fori_loop(0, CL_DEV, take_halo_b, 0)
+    take_halo(0, halo_b)
     base = me * CL_DEV - 8
 
     def near_term(q):
@@ -343,21 +350,13 @@
 
         lax.fori_loop(0, CL_DEV, step, 0)
 
-    def take_halo(q):
-        def step(j, carry):
-            put(q, lax.rem(j + 24, 32), halo_u[q, lax.div(j, 2), lax.rem(j, 2)])
-            return carry
-
-        lax.fori_loop(0, CL_DEV, step, 0)
-
-    def halo_pass(q):
-        halo_copy(q + 1).wait_recv()
-        gather_start(q + 3)
-
     finish_rows(0)
     rows_start(0)
+    rows_send(0)
+    gather_forward(5)
+    gather_end(5)
+    take_halo(1, halo_b)
     near_term(1)
-    rows_send(0)
     rows_own(0)
     halo_copy(1).start()
     gather_start(1)
@@ -365,24 +364,26 @@
     gather_end(1)
     take_own(0)
     send_coefficients(1, 0)
-    halo_pass(0)
 
     far_term(0, 1, 0, n_rows)
     finish_rows(1)
     rows_start(1)
     rows_send(1)
-    gather_forward(3)
+    halo_copy(1).wait_recv()
     rows_own(1)
     halo_copy(2).start()
     gather_start(2)
+    gather_start(3)
     gather_forward(2)
     gather_end(2)
     take_own(1)
     send_coefficients(1, 1)
+    gather_forward(3)
+    halo_copy(2).wait_recv()
+    gather_start(4)
     gather_end(3)
-    take_halo(0)
+    take_halo(0, halo_u)
     near_term(0)
-    halo_pass(1)
 
     def finish_columns(q, h):
         def step(g, carry):
@@ -429,7 +430,7 @@
         columns_sib(0, h).wait_recv()
         columns_send(0, h)
     gather_end(4)
-    take_halo(1)
+    take_halo(1, halo_u)
     near_term(1)
     my_half = lax.rem(my_y, 2)
 
@@ -442,6 +443,21 @@
     lax.fori_loop(0, CL_DEV, turn, 0)
     for h in range(2):
         columns_own(0, h)
+    mine = pl.ds(pl.multiple_of((lax.div(my_y, 2) * 2 + my_c) * 32, 32), 32)
+    lane = lax.broadcasted_iota(jnp.int32, (32, B), 1)
+
+    def dots(pairs):
+        def step(o, sums):
+            lanes = pl.ds(pl.multiple_of(o * B, B), B)
+            items = (turned[0, mine, lanes], turned[1, mine, lanes], own_w[:, lanes] if pairs[-1][1] == 2 else None)
+            return tuple(total + items[i] * items[j] for total, (i, j) in zip(sums, pairs))
+
+        sums = lax.fori_loop(0, CL_DEV, step, tuple(jnp.zeros((32, B), F32) for _ in pairs))
+        return [jnp.sum(item, axis=1, keepdims=True) for item in sums]
+
+    early = dots(((0, 0), (0, 1), (1, 1)))
+    for q in range(2):
+        lax.fori_loop(1, n_rows, lambda k, carry: settle(0, q, k), 0)
     far_term(1, 1, 0, n_rows)
     for h in range(2):
         finish_columns(1, h)
@@ -449,21 +465,14 @@
     for h in range(2):
         columns_sib(1, h).wait_recv()
         columns_send(1, h)
+    for q in range(2):
+        lax.fori_loop(1, n_rows, lambda k, carry: settle(1, q, k), 0)
     for h in range(2):
         columns_own(1, h)
 
-    mine = pl.ds(pl.multiple_of((lax.div(my_y, 2) * 2 + my_c) * 32, 32), 32)
-    lane = lax.broadcasted_iota(jnp.int32, (32, B), 1)
-
-    def dots(o, sums):
-        lanes = pl.ds(pl.multiple_of(o * B, B), B)
-        b, u, w = turned[0, mine, lanes], turned[1, mine, lanes], own_w[:, lanes]
-        return tuple(total + item for total, item in zip(sums, (b * b, b * u, u * u, b * w, u * w, w * w)))
-
-    sums = lax.fori_loop(0, CL_DEV, dots, tuple(jnp.zeros((32, B), F32) for _ in range(6)))
     table = jnp.zeros((32, B), F32)
-    for j in range(6):
-        table = jnp.where(lane == j, jnp.sum(sums[j], axis=1, keepdims=True), table)
+    for j, item in enumerate(early + dots(((0, 2), (1, 2), (2, 2)))):
+        table = jnp.where(lane == j, item, table)
     flat = jnp.concatenate([table, jnp.zeros((B - 32, B), F32)], axis=0).T[:8]
     gram_out[...] = flat
 
@@ -472,6 +481,10 @@
 
     def gram_start(k, carry):
         gram(k).start()
+        return carry
+
+    def gram_settle(k, carry):
+        gram(k).wait_send()
         return carry
 
     lax.fori_loop(1, n_rows, gram_start, 0)
@@ -489,17 +502,10 @@
     sol_ref[...] = parts[0] * b + parts[1] * u
     res_ref[...] = parts[2] * b + parts[3] * u + parts[4] * w
 
-    def settle(k, carry):
-        for ap in range(2):
-            for q in range(2):
-                a2a(ap, q, k).wait_send()
-        gram(k).wait_send()
-        return carry
-
-    lax.fori_loop(1, n_rows, settle, 0)
-    for g in range(3):
+    lax.fori_loop(1, n_rows, gram_settle, 0)
+    for g in (1, 2, 3, 4):
         halo_copy(g).wait_send()
-    for g in range(5):
+    for g in range(6):
         for d in range(FAR_Y):
             if d > 0:
                 gather_y(g, d).wait_send()
@@ -517,12 +523,9 @@
                     columns_y(q, h, j).wait_send()
 
 
-def deliver(sol_in, res_in, sol_out, res_out, sem):
-    copies = [pltpu.make_async_copy(sol_in, sol_out, sem.at[0]), pltpu.make_async_copy(res_in, res_out, sem.at[1])]
-    for copy in copies:
-        copy.start()
-    for copy in copies:
-        copy.wait()
+def deliver(sol_in, res_in, sol_out, res_out):
+    sol_out[...] = sol_in[...]
+    res_out[...] = res_in[...]
 
 
 def solution(mesh):
@@ -549,7 +552,7 @@
                 pltpu.VMEM((2, 32, B, 2 * HALF), BF16),
                 pltpu.VMEM((2, 2, n_rows, R, HALF), F32),
                 pltpu.VMEM((2, 2, n_rows, R, HALF), F32),
-                pltpu.VMEM((8, 2, B, 2 * HALF), F32),
+                pltpu.VMEM((2, 8, 2, B, HALF), F32),
                 pltpu.VMEM((2, 8, 2, B, HALF), F32),
                 pltpu.VMEM((2, 8, 2, B, HALF), F32),
                 pltpu.VMEM((2, CL_DEV, B, HALF), F32),
@@ -568,8 +571,8 @@
                 pltpu.VMEM((n_rows, 8, B), F32),
                 pltpu.SMEM((n_rows,), jnp.int32),
                 pltpu.SMEM((CL_DEV,), jnp.int32),
-                dma((4,)), dma((2, 2, n_rows)), dma((2, 2, n_rows)), dma((3,)), dma((3,)),
-                dma((5, 4)), dma((5, 4)), dma((5, 4)), dma((5, 4)),
+                dma((4,)), dma((2, 2, n_rows)), dma((2, 2, n_rows)), dma((5,)), dma((5,)),
+                dma((6, 4)), dma((6, 4)), dma((6, 4)), dma((6, 4)),
                 dma((2, 4)), dma((2, 4)), dma((2, 4)), dma((2, 4)),
                 dma((2, 2)), dma((2, 2)), dma((2, 2, 2)), dma((2, 4)),
                 dma((n_rows,)), dma((n_rows,)),
@@ -588,9 +591,8 @@
         sol, res = pl.pallas_call(
             deliver,
             out_shape=(jax.ShapeDtypeStruct((32, CL_DEV * B), F32),) * 2,
-            in_specs=[anywhere] * 2,
-            out_specs=(anywhere, anywhere),
-            scratch_shapes=[dma((2,))],
+            in_specs=[vector] * 2,
+            out_specs=(vector, vector),
             name="deliver",
         )(sol, res)
         return sol.T, res.T

time: 168 us -> 151 us (0.90); the launches traced: 168 us -> 148 us
  Pallas kernels: 167 us -> 148 us
    pallas_call x1, Pallas kernels: 17 us -> 1.84 us  [shards(): pl.pallas_call(deliver, out_shape=(jax.ShapeDtypeStruct((32, CL_DEV * B),...]
    pallas_call x1, Pallas kernels: 150 us -> 146 us  [shards(): pl.pallas_call(functools.partial(kernel, n_rows), out_shape=(jax.ShapeDty...]
where the time goes in v4:
time: 151 us; the launch traced here: 148 us
  Pallas kernels  148 us (98%)
    pallas_call x1, Pallas kernels, shards(): pl.pallas_call(functools.partial(kernel, n_rows), out_shape=(jax.ShapeDty...  146 us

profile of v4, /device:TPU:24, one launch (start us, length us, event | category | flops | bytes accessed | tf_op | source)
XLA Modules:
  0.0 148.3 jit_solution(9059971735295610318)
XLA Ops:
  0.6 145.9 %gmres.1 = (f32[32,2048]{1,0:T(8,128)}, f32[32,2048]{1,0:T(8,128)}) custom-call(s32[6,16]{1,0:T(8,128)} %bitcast.15, s32[32]{0:T(128)} %bitcast.16, s32[32]{0:T(128)} %bitcast.17, f32[16,128,256]{2,1,0:T(8,128)} %bitcast.12, f32[16,6,128,128]{3,2,1,0:T(8,128)} %near_hbm.1, f32[32,64,128]{2,1,0:T(8,128)} %bitcast.13, f32[32,64,128]{2,1,0:T(8,128)} %bitcast.14), custom_call_target="tpu_custom_call" | custom-call | tf_op jit(solution)/shard_map/gmres/pallas_call | solution.py:539
  146.5 1.8 %deliver.1 = (f32[32,2048]{1,0:T(8,128)}, f32[32,2048]{1,0:T(8,128)}) custom-call(f32[32,2048]{1,0:T(8,128)} %get-tuple-element.6.sol_in, f32[32,2048]{1,0:T(8,128)} %get-tuple-element.7.res_in), custom_call_target="tpu_custom_call" | custom-call | tf_op jit(solution)/shard_map/deliver/pallas_call | solution.py:591

commit v5 on v4

--- a/solution.py
+++ b/solution.py
@@ -467,42 +467,6 @@
         columns_send(1, h)
     for q in range(2):
         lax.fori_loop(1, n_rows, lambda k, carry: settle(1, q, k), 0)
-    for h in range(2):
-        columns_own(1, h)
-
-    table = jnp.zeros((32, B), F32)
-    for j, item in enumerate(early + dots(((0, 2), (1, 2), (2, 2)))):
-        table = jnp.where(lane == j, item, table)
-    flat = jnp.concatenate([table, jnp.zeros((B - 32, B), F32)], axis=0).T[:8]
-    gram_out[...] = flat
-
-    def gram(k):
-        return remote(gram_out, gram_in.at[k], gram_s.at[k], gram_r.at[k], ahead(k), far)
-
-    def gram_start(k, carry):
-        gram(k).start()
-        return carry
-
-    def gram_settle(k, carry):
-        gram(k).wait_send()
-        return carry
-
-    lax.fori_loop(1, n_rows, gram_start, 0)
-    gram_in[0] = flat
-
-    def gram_add(k, total):
-        gram(k).wait_recv()
-        return total + gram_in[k]
-
-    total = lax.fori_loop(1, n_rows, gram_add, gram_in[0])
-    weights = combine([total[j : j + 1] for j in range(6)])
-    stack = jnp.concatenate(list(weights) + [jnp.zeros((B - 5, B), F32)], axis=0).T
-    parts = [stack[:32, j : j + 1] for j in range(5)]
-    b, u, w = turned[0, mine, :], turned[1, mine, :], own_w[...]
-    sol_ref[...] = parts[0] * b + parts[1] * u
-    res_ref[...] = parts[2] * b + parts[3] * u + parts[4] * w
-
-    lax.fori_loop(1, n_rows, gram_settle, 0)
     for g in (1, 2, 3, 4):
         halo_copy(g).wait_send()
     for g in range(6):
@@ -517,10 +481,53 @@
             rows_y(q, d).wait_send()
         for h in range(2):
             columns_sib(q, h).wait_send()
-            for j in range(2):
-                @pl.when(my_y != q + 2 * j)
-                def _():
-                    columns_y(q, h, j).wait_send()
+    for h in range(2):
+        for j in range(2):
+            @pl.when(my_y != 2 * j)
+            def _():
+                columns_y(0, h, j).wait_send()
+    for h in range(2):
+        columns_own(1, h)
+
+    table = jnp.zeros((32, B), F32)
+    for j, item in enumerate(early + dots(((0, 2), (1, 2), (2, 2)))):
+        table = jnp.where(lane == j, item, table)
+    flat = jnp.concatenate([table, jnp.zeros((B - 32, B), F32)], axis=0).T[:8]
+    gram_out[0] = flat
+
+    def gram(k):
+        return remote(gram_out.at[0 if k < ROW_X else 1], gram_in.at[k], gram_s.at[k], gram_r.at[k], ahead(k), far)
+
+    along_x = list(range(1, ROW_X))
+    along_z = [ROW_X * dz for dz in range(1, n_z)]
+    total = flat
+    for k in along_x:
+        gram(k).start()
+    for k in along_x:
+        gram(k).wait_recv()
+    for k in along_x:
+        total = total + gram_in[k]
+    gram_out[1] = total
+    for k in along_z:
+        gram(k).start()
+    for k in along_z:
+        gram(k).wait_recv()
+    for k in along_z:
+        total = total + gram_in[k]
+    weights = combine([total[j : j + 1] for j in range(6)])
+    stack = jnp.concatenate(list(weights) + [jnp.zeros((B - 5, B), F32)], axis=0).T
+    parts = [stack[:32, j : j + 1] for j in range(5)]
+    b, u, w = turned[0, mine, :], turned[1, mine, :], own_w[...]
+    sol_ref[...] = parts[0] * b + parts[1] * u
+    res_ref[...] = parts[2] * b + parts[3] * u + parts[4] * w
+
+    for k in along_x + along_z:
+        gram(k).wait_send()
+    for h in range(2):
+        for j in range(2):
+            @pl.when(my_y != 1 + 2 * j)
+            def _():
+                columns_y(1, h, j).wait_send()
 
 
 def deliver(sol_in, res_in, sol_out, res_out):
@@ -567,7 +574,7 @@
                 pltpu.VMEM((2, 4, 32, ROW_HALF), F32),
                 pltpu.VMEM((2, HALF, CL_DEV * B), F32),
                 pltpu.VMEM((32, CL_DEV * B), F32),
-                pltpu.VMEM((8, B), F32),
+                pltpu.VMEM((2, 8, B), F32),
                 pltpu.VMEM((n_rows, 8, B), F32),
                 pltpu.SMEM((n_rows,), jnp.int32),
                 pltpu.SMEM((CL_DEV,), jnp.int32),

time: 151 us -> 151 us (level)
  no operation moved by 1% of the time
where the time goes in v5:
time: 151 us; the launch traced here: 149 us
  Pallas kernels  149 us (99%)
    pallas_call x1, Pallas kernels, shards(): pl.pallas_call(functools.partial(kernel, n_rows), out_shape=(jax.ShapeDty...  147 us

profile of v5, /device:TPU:24, one launch (start us, length us, event | category | flops | bytes accessed | tf_op | source)
XLA Modules:
  0.0 149.4 jit_solution(13175331264051749894)
XLA Ops:
  0.6 146.9 %gmres.1 = (f32[32,2048]{1,0:T(8,128)}, f32[32,2048]{1,0:T(8,128)}) custom-call(s32[6,16]{1,0:T(8,128)} %bitcast.15, s32[32]{0:T(128)} %bitcast.16, s32[32]{0:T(128)} %bitcast.17, f32[16,128,256]{2,1,0:T(8,128)} %bitcast.12, f32[16,6,128,128]{3,2,1,0:T(8,128)} %near_hbm.1, f32[32,64,128]{2,1,0:T(8,128)} %bitcast.13, f32[32,64,128]{2,1,0:T(8,128)} %bitcast.14), custom_call_target="tpu_custom_call" | custom-call | tf_op jit(solution)/shard_map/gmres/pallas_call | solution.py:546
  147.5 1.8 %deliver.1 = (f32[32,2048]{1,0:T(8,128)}, f32[32,2048]{1,0:T(8,128)}) custom-call(f32[32,2048]{1,0:T(8,128)} %get-tuple-element.6.sol_in, f32[32,2048]{1,0:T(8,128)} %get-tuple-element.7.res_in), custom_call_target="tpu_custom_call" | custom-call | tf_op jit(solution)/shard_map/deliver/pallas_call | solution.py:598

commit v6 on v5

--- a/solution.py
+++ b/solution.py
@@ -157,16 +157,24 @@
     lax.fori_loop(0, n_rows, take_right, 0)
     pl.semaphore_wait(barrier, n_rows + 3)
 
-    halo_to = lax.rem(me + n_rows - 1 + 2 * lax.div(far, 4), n_rows)
-
-    def halo_copy(g):
+    halo_to = (lax.rem(me + n_rows - 1, n_rows), lax.rem(me + 1, n_rows))
+
+    def halo_copy(g, i):
         if g >= 3:
-            rows = side.at[pl.ds(2 * far, 2), :, pl.ds((g - 3) * HALF, HALF)]
-            return remote(rows, halo_b.at[g - 3, far], halo_s.at[g], halo_r.at[g], halo_to, far)
-        return remote(own_u.at[g - 1, far], halo_u.at[g - 1, far], halo_s.at[g], halo_r.at[g], halo_to, far)
-
-    halo_copy(3).start()
-    halo_copy(4).start()
+            rows = side.at[far + 8 * i, :, pl.ds((g - 3) * HALF, HALF)]
+            return remote(rows, halo_b.at[g - 3, far, i], halo_s.at[g, i], halo_r.at[g, i], halo_to[i], far)
+        return remote(own_u.at[g - 1, far, i], halo_u.at[g - 1, far, i], halo_s.at[g, i], halo_r.at[g, i], halo_to[i], far)
+
+    def halo_start(g):
+        for i in range(2):
+            halo_copy(g, i).start()
+
+    def halo_wait(g):
+        for i in range(2):
+            halo_copy(g, i).wait_recv()
+
+    halo_start(3)
+    halo_start(4)
 
     def a2a(ap, q, k):
         return remote(coef_out.at[ap, q, k], coef_in.at[ap, q, k], a2a_s.at[ap, q, k], a2a_r.at[ap, q, k], ahead(k), far)
@@ -226,7 +234,7 @@
             remote(ref, ref, ags_s.at[g, d], ags_r.at[g, d], me, sib).wait_recv()
 
     for q in range(2):
-        halo_copy(q + 3).wait_recv()
+        halo_wait(q + 3)
         gather_start(q * 5)
 
     def tables(k, carry):
@@ -272,7 +280,8 @@
 
     def take_halo(q, halo):
         def step(j, carry):
-            put(q, lax.rem(j + 24, 32), halo[q, lax.div(j, 2), lax.rem(j, 2)])
+            who, i = lax.rem(j, 8), lax.div(j, 8)
+            put(q, who + 24 * (1 - i), halo[q, who, i])
             return carry
 
         lax.fori_loop(0, CL_DEV, step, 0)
@@ -315,14 +324,14 @@
 
     def finish_rows(q):
         def step(o, carry):
-            part[q, lax.div(o, 4), lax.rem(lax.div(o, 2), 2), lax.rem(o, 2)] = acc[q, o] + chain[last[o]]
+            part[q, lax.div(o, 8), lax.rem(lax.div(o, 2), 4), lax.rem(o, 2)] = acc[q, o] + chain[last[o]]
             return carry
 
         lax.fori_loop(0, CL_DEV, step, 0)
 
     def rows_sib(q, d):
         to_y = lax.rem(my_y + d, FAR_Y)
-        return remote(part.at[q, to_y, 1 - my_c], sib_in.at[q, d], rss_s.at[q, d], rss_r.at[q, d], me, sib)
+        return remote(part.at[q, :, to_y, 1 - my_c], sib_in.at[q, d], rss_s.at[q, d], rss_r.at[q, d], me, sib)
 
     def rows_y(q, d):
         return remote(mix.at[q, d], y_in.at[q, d], rsy_s.at[q, d], rsy_r.at[q, d], me, y_peer(d))
@@ -334,18 +343,18 @@
     def rows_send(q):
         for d in (2, 1, 3):
             rows_sib(q, d).wait_recv()
-            mix[q, d] = part[q, lax.rem(my_y + d, FAR_Y), my_c] + sib_in[q, d]
+            mix[q, d] = part[q, :, lax.rem(my_y + d, FAR_Y), my_c] + sib_in[q, d]
             rows_y(q, d).start()
         rows_sib(q, 0).wait_recv()
 
     def rows_own(q):
         for d in (1, 2, 3):
             rows_y(q, d).wait_recv()
-        own_u[q, far] = (part[q, my_y, my_c] + sib_in[q, 0]) + (y_in[q, 1] + y_in[q, 2] + y_in[q, 3])
+        own_u[q, far] = (part[q, :, my_y, my_c] + sib_in[q, 0]) + (y_in[q, 1] + y_in[q, 2] + y_in[q, 3])
 
     def take_own(q):
         def step(j, carry):
-            put(q, j + 8, own_u[q, lax.div(j, 2), lax.rem(j, 2)])
+            put(q, j + 8, own_u[q, lax.rem(j, 8), lax.div(j, 8)])
             return carry
 
         lax.fori_loop(0, CL_DEV, step, 0)
@@ -358,7 +367,7 @@
     take_halo(1, halo_b)
     near_term(1)
     rows_own(0)
-    halo_copy(1).start()
+    halo_start(1)
     gather_start(1)
     gather_forward(1)
     gather_end(1)
@@ -369,9 +378,9 @@
     finish_rows(1)
     rows_start(1)
     rows_send(1)
-    halo_copy(1).wait_recv()
+    halo_wait(1)
     rows_own(1)
-    halo_copy(2).start()
+    halo_start(2)
     gather_start(2)
     gather_start(3)
     gather_forward(2)
@@ -379,7 +388,7 @@
     take_own(1)
     send_coefficients(1, 1)
     gather_forward(3)
-    halo_copy(2).wait_recv()
+    halo_wait(2)
     gather_start(4)
     gather_end(3)
     take_halo(0, halo_u)
@@ -437,7 +446,7 @@
     def turn(o, carry):
         lanes = pl.ds(pl.multiple_of(o * B, B), B)
         turned[0, :, lanes] = side[o, :, pl.ds(pl.multiple_of(my_half * HALF, HALF), HALF)].T
-        turned[1, :, lanes] = own_u[my_half, lax.div(o, 2), lax.rem(o, 2)].T
+        turned[1, :, lanes] = own_u[my_half, lax.rem(o, 8), lax.div(o, 8)].T
         return carry
 
     lax.fori_loop(0, CL_DEV, turn, 0)
@@ -468,7 +477,8 @@
     for q in range(2):
         lax.fori_loop(1, n_rows, lambda k, carry: settle(1, q, k), 0)
     for g in (1, 2, 3, 4):
-        halo_copy(g).wait_send()
+        for i in range(2):
+            halo_copy(g, i).wait_send()
     for g in range(6):
         for d in range(FAR_Y):
             if d > 0:
@@ -564,7 +574,7 @@
                 pltpu.VMEM((2, 8, 2, B, HALF), F32),
                 pltpu.VMEM((2, CL_DEV, B, HALF), F32),
                 pltpu.VMEM((n_rows + 1, B, HALF), F32),
-                pltpu.VMEM((2, 4, 2, 2, B, HALF), F32),
+                pltpu.VMEM((2, 2, 4, 2, B, HALF), F32),
                 pltpu.VMEM((2, 2, 2, 2, 32, ROW_HALF), F32),
                 pltpu.VMEM((2, 4, 2, B, HALF), F32),
                 pltpu.VMEM((2, 4, 2, B, HALF), F32),
@@ -578,7 +588,7 @@
                 pltpu.VMEM((n_rows, 8, B), F32),
                 pltpu.SMEM((n_rows,), jnp.int32),
                 pltpu.SMEM((CL_DEV,), jnp.int32),
-                dma((4,)), dma((2, 2, n_rows)), dma((2, 2, n_rows)), dma((5,)), dma((5,)),
+                dma((4,)), dma((2, 2, n_rows)), dma((2, 2, n_rows)), dma((5, 2)), dma((5, 2)),
                 dma((6, 4)), dma((6, 4)), dma((6, 4)), dma((6, 4)),
                 dma((2, 4)), dma((2, 4)), dma((2, 4)), dma((2, 4)),
                 dma((2, 2)), dma((2, 2)), dma((2, 2, 2)), dma((2, 4)),

time: 151 us -> 147 us (0.974)
  Pallas kernels: 149 us -> 145 us
    pallas_call x1, Pallas kernels: 147 us -> 143 us  [shards(): pl.pallas_call(functools.partial(kernel, n_rows), out_shape=(jax.ShapeDty...]
where the time goes in v6:
time: 147 us; the launch traced here: 146 us
  Pallas kernels  145 us (99%)
    pallas_call x1, Pallas kernels, shards(): pl.pallas_call(functools.partial(kernel, n_rows), out_shape=(jax.ShapeDty...  143 us

profile of v6, /device:TPU:24, one launch (start us, length us, event | category | flops | bytes accessed | tf_op | source)
XLA Modules:
  0.0 145.8 jit_solution(13790017503947026317)
XLA Ops:
  0.6 143.3 %gmres.1 = (f32[32,2048]{1,0:T(8,128)}, f32[32,2048]{1,0:T(8,128)}) custom-call(s32[6,16]{1,0:T(8,128)} %bitcast.15, s32[32]{0:T(128)} %bitcast.16, s32[32]{0:T(128)} %bitcast.17, f32[16,128,256]{2,1,0:T(8,128)} %bitcast.12, f32[16,6,128,128]{3,2,1,0:T(8,128)} %near_hbm.1, f32[32,64,128]{2,1,0:T(8,128)} %bitcast.13, f32[32,64,128]{2,1,0:T(8,128)} %bitcast.14), custom_call_target="tpu_custom_call" | custom-call | tf_op jit(solution)/shard_map/gmres/pallas_call | solution.py:556
  143.9 1.8 %deliver.1 = (f32[32,2048]{1,0:T(8,128)}, f32[32,2048]{1,0:T(8,128)}) custom-call(f32[32,2048]{1,0:T(8,128)} %get-tuple-element.6.sol_in, f32[32,2048]{1,0:T(8,128)} %get-tuple-element.7.res_in), custom_call_target="tpu_custom_call" | custom-call | tf_op jit(solution)/shard_map/deliver/pallas_call | solution.py:608
